TPU v7x, 32 devices: a whole 2x2x4 slice. The times are simulated.
32 devices in a mesh: grid: 8 (over z, core), vec: 4 (over y, x).
Axes of the slice: x: 2, y: 2, z: 4, core: 2. Of those that a mesh axis runs over, the one named last changes fastest.
Arguments:
- orbitals: bfloat16 [884736, 512], P(('grid', 'vec')), may hold values from -1.296875 to 1.296875
- inverse_panel: bfloat16 [2048, 32], replicated, may hold values from -0.125 to 0.125
- points: int32 [2048], replicated, may hold values from 0 to 884735, as said below
Outputs:
- projected: float32 [2048, 32], P(('grid', 'vec'))
Inputs may be any that keep to these rules, and one draw needn't show every extreme that they name: `points`: distinct cell indices.
All inputs are finite; a program needn't handle non-finite values.
Results may differ from a plain program's by a relative error of at most 0.005.
Values may be sent and summed in bfloat16 or wider, within the bound.
A program may use at most 256 MiB of HBM per device.

v0:
```python
import math

import jax
import jax.numpy as jnp
from jax import lax
from jax.experimental import pallas as pl
from jax.experimental.pallas import tpu as pltpu
from jax.sharding import PartitionSpec as P

NG = 96


SCREEN = 2.25


def wave_tables(count):
    index = lax.iota(jnp.int32, count)
    phase = index[:, None] * index[None, :] % count
    angle = phase.astype(jnp.float32) * (2.0 * math.pi / count)
    return (jnp.cos(angle).astype(jnp.bfloat16), jnp.sin(angle).astype(jnp.bfloat16))


def wavenumber(index, count):
    return jnp.where(index < count // 2, index, index - count).astype(jnp.float32)


def screened(wave_x, wave_y, wave_z):
    squared = (
        wave_x[:, None, None] * wave_x[:, None, None]
        + wave_y[None, :, None] * wave_y[None, :, None]
        + wave_z[None, None, :] * wave_z[None, None, :]
    )
    factor = NG / (2.0 * math.pi) * (NG / (2.0 * math.pi))
    return jnp.where(squared > 0.5, factor / (squared + SCREEN), jnp.float32(0.0))


def mult(data, table, form):
    return jnp.einsum(form, data, table, preferred_element_type=jnp.float32)


LANES = 128


def exchange_kernel(axes, total, gather, x_ref, o_ref, held, send_sem, recv_sem, own_sem):
    if len(axes) == 2:
        vec_count = lax.axis_size("vec")
        count = lax.axis_size("grid") * vec_count
        me = lax.axis_index("grid") * vec_count + lax.axis_index("vec")
    else:
        count = lax.axis_size(axes[0])
        me = lax.axis_index(axes[0])
    land = held if total else o_ref

    def place(index):
        if len(axes) == 2:
            return (index // vec_count, lax.rem(index, vec_count))
        if axes[0] == "grid":
            return (index, lax.axis_index("vec"))
        return (lax.axis_index("grid"), index)

    def part(index):
        return x_ref if gather else x_ref.at[index]

    barrier = pltpu.get_barrier_semaphore()

    def greet(step, carry):
        pl.semaphore_signal(
            barrier,
            inc=1,
            device_id=place(lax.rem(me + step, count)),
            device_id_type=pl.DeviceIdType.MESH,
        )
        return carry

    lax.fori_loop(1, count, greet, 0)
    own = pltpu.make_async_copy(part(me), land.at[me], own_sem)
    own.start()
    pl.semaphore_wait(barrier, count - 1)

    def copy(step, source, slot):
        peer = lax.rem(me + step, count)
        return pltpu.make_async_remote_copy(
            src_ref=part(source),
            dst_ref=land.at[slot],
            send_sem=send_sem.at[step],
            recv_sem=recv_sem.at[step],
            device_id=place(peer),
            device_id_type=pl.DeviceIdType.MESH,
        )

    def send(step, carry):
        copy(step, lax.rem(me + step, count), me).start()
        return carry

    lax.fori_loop(1, count, send, 0)
    own.wait()

    def receive(step, carry):
        source = lax.rem(me + count - step, count)
        copy(step, source, source).wait_recv()
        return carry

    lax.fori_loop(1, count, receive, 0)
    if total:
        o_ref[...] = jnp.sum(held[...].astype(jnp.float32), axis=0).astype(o_ref.dtype)

    def drain(step, carry):
        copy(step, lax.rem(me + step, count), me).wait_send()
        return carry

    lax.fori_loop(1, count, drain, 0)


def exchange(blocks, ident, total=False, axes=("grid", "vec"), gather=False):
    rows, lanes = blocks.shape[-2:]
    count = 1
    for axis in axes:
        count *= lax.axis_size(axis)
    shape = (rows, lanes) if total else (count, rows, lanes)
    held_shape = blocks.shape if total else (1, 8, LANES)

    def body(*refs):
        exchange_kernel(axes, total, gather, *refs)

    return pl.pallas_call(
        body,
        out_shape=jax.ShapeDtypeStruct(shape, blocks.dtype),
        in_specs=[pl.BlockSpec(memory_space=pltpu.VMEM)],
        out_specs=pl.BlockSpec(memory_space=pltpu.VMEM),
        scratch_shapes=[
            pltpu.VMEM(held_shape, blocks.dtype),
            pltpu.SemaphoreType.DMA((count,)),
            pltpu.SemaphoreType.DMA((count,)),
            pltpu.SemaphoreType.DMA(()),
        ],
        compiler_params=pltpu.CompilerParams(
            collective_id=ident, has_side_effects=True, vmem_limit_bytes=32 << 20
        ),
        name="exchange_total" if total else "exchange_gather" if gather else "exchange_blocks",
    )(blocks)


def share_rows(picked, grid_count, vec_count):
    npoints, norb = picked.shape
    if npoints % (grid_count * vec_count * 16) != 0:
        return lax.psum(picked.astype(jnp.float32), ("grid", "vec")).astype(picked.dtype)
    mine = exchange(
        picked.reshape(vec_count, npoints // vec_count, norb), 4, total=True, axes=("vec",)
    )
    mine = exchange(
        mine.reshape(grid_count, npoints // vec_count // grid_count, norb),
        5,
        total=True,
        axes=("grid",),
    )
    block = exchange(mine, 6, axes=("grid",), gather=True).reshape(npoints // vec_count, norb)
    return exchange(block, 7, axes=("vec",), gather=True).reshape(npoints, norb)


def transform(re, im, cos_tab, sin_tab, form, sign):
    out_re = mult(re, cos_tab, form) + sign * mult(im, sin_tab, form)
    out_im = mult(im, cos_tab, form) - sign * mult(re, sin_tab, form)
    return out_re, out_im


def solve_columns(fit_cols):
    bf = jnp.bfloat16
    count = fit_cols.shape[0]
    rows = fit_cols.shape[1]
    flat = exchange(fit_cols.reshape(count, rows // LANES, LANES), 1)
    field = flat.reshape(1, NG, NG, NG)
    cos_tab, sin_tab = wave_tables(NG)
    waves = wavenumber(lax.iota(jnp.int32, NG), NG)
    kernel = screened(waves, waves, waves)[None]
    a_re = mult(field, cos_tab, "vxyz,zk->vxyk").astype(bf)
    a_im = (-mult(field, sin_tab, "vxyz,zk->vxyk")).astype(bf)
    b_re, b_im = transform(a_re, a_im, cos_tab, sin_tab, "vxyz,yk->vxkz", 1.0)
    b_re, b_im = b_re.astype(bf), b_im.astype(bf)
    h_re, h_im = transform(b_re, b_im, cos_tab, sin_tab, "vxyz,xk->vkyz", 1.0)
    q_re, q_im = (h_re * kernel).astype(bf), (h_im * kernel).astype(bf)
    g_re, g_im = transform(q_re, q_im, cos_tab, sin_tab, "vxyz,xk->vkyz", -1.0)
    g_re, g_im = g_re.astype(bf), g_im.astype(bf)
    p_re, p_im = transform(g_re, g_im, cos_tab, sin_tab, "vxyz,yk->vxkz", -1.0)
    p_re, p_im = p_re.astype(bf), p_im.astype(bf)
    final = mult(p_re, cos_tab, "vxyz,zk->vxyk") - mult(p_im, sin_tab, "vxyz,zk->vxyk")
    potential = (final / float(NG**3)).astype(bf).reshape(flat.shape)
    return exchange(potential, 2).reshape(count, rows)


def project(pair, pot_rows):
    scale = 1.0 / math.sqrt(float(NG**3))
    term = lax.dot_general(
        pair, pot_rows, (((0,), (1,)), ((), ())), preferred_element_type=jnp.float32
    )
    term = term * jnp.float32(scale)
    npoints, cols = term.shape
    count = lax.axis_size("grid") * lax.axis_size("vec")
    share = npoints // count
    if share * cols % LANES == 0:
        blocks = term.reshape(count, share * cols // LANES, LANES)
        return exchange(blocks, 3, True).reshape(share, cols)
    partial_block = lax.psum_scatter(term, "grid", scatter_dimension=0, tiled=True)
    return lax.psum_scatter(partial_block, "vec", scatter_dimension=0, tiled=True)


def shards(orbitals, inverse_panel, points):
    bf = jnp.bfloat16
    row_count = orbitals.shape[0]
    grid_count = lax.axis_size("grid")
    vec_count = lax.axis_size("vec")
    npoints = points.shape[0]
    offset = (lax.axis_index("grid") * vec_count + lax.axis_index("vec")) * row_count
    local_pos = points - offset
    inside = (local_pos >= 0) & (local_pos < row_count)
    picked = jnp.take(orbitals, jnp.clip(local_pos, 0, row_count - 1), axis=0)
    picked = jnp.where(inside[:, None], picked, jnp.zeros_like(picked))
    point_rows = share_rows(picked, grid_count, vec_count)

    def pair_block(block):
        correlation = lax.dot_general(
            block, point_rows, (((1,), (1,)), ((), ())), preferred_element_type=jnp.float32
        )
        return (correlation * correlation).astype(bf)

    pair = lax.map(pair_block, orbitals.reshape(4, row_count // 4, orbitals.shape[1])).reshape(
        row_count, npoints
    )
    fit_cols = lax.dot_general(
        inverse_panel, pair, (((0,), (1,)), ((), ())), preferred_element_type=jnp.float32
    ).astype(bf)
    if inverse_panel.shape[1] == grid_count * vec_count and row_count % LANES == 0:
        return project(pair, solve_columns(fit_cols))
    slab = lax.all_to_all(fit_cols, "vec", split_axis=0, concat_axis=1, tiled=True)
    col_local = slab.shape[0]
    planes = NG // grid_count
    field = slab.reshape(col_local, planes, NG, NG)
    cos_tab, sin_tab = wave_tables(NG)
    z_re = mult(field, cos_tab, "vxyz,zk->vxyk").astype(bf)
    z_im = (-mult(field, sin_tab, "vxyz,zk->vxyk")).astype(bf)
    y_re = (mult(z_re, cos_tab, "vxyz,yk->vxkz") + mult(z_im, sin_tab, "vxyz,yk->vxkz")).astype(bf)
    y_im = (mult(z_im, cos_tab, "vxyz,yk->vxkz") - mult(z_re, sin_tab, "vxyz,yk->vxkz")).astype(bf)
    stacked = jnp.stack([y_re, y_im])
    waves = wavenumber(lax.iota(jnp.int32, NG), NG)
    y_waves = wavenumber(lax.axis_index("grid") * planes + lax.iota(jnp.int32, planes), NG)
    kernel = screened(waves, y_waves, waves)[None]
    piece = lax.all_to_all(stacked, "grid", split_axis=3, concat_axis=2, tiled=True)
    p_re = piece[0]
    p_im = piece[1]
    x_re = mult(p_re, cos_tab, "vxyz,xk->vkyz") + mult(p_im, sin_tab, "vxyz,xk->vkyz")
    x_im = mult(p_im, cos_tab, "vxyz,xk->vkyz") - mult(p_re, sin_tab, "vxyz,xk->vkyz")
    q_re = (x_re * kernel).astype(bf)
    q_im = (x_im * kernel).astype(bf)
    i_re = (mult(q_re, cos_tab, "vxyz,xk->vkyz") - mult(q_im, sin_tab, "vxyz,xk->vkyz")).astype(bf)
    i_im = (mult(q_im, cos_tab, "vxyz,xk->vkyz") + mult(q_re, sin_tab, "vxyz,xk->vkyz")).astype(bf)
    spectrum = lax.all_to_all(
        jnp.stack([i_re, i_im]), "grid", split_axis=2, concat_axis=3, tiled=True
    )
    s_re = spectrum[0]
    s_im = spectrum[1]
    h_re = (mult(s_re, cos_tab, "vxyz,yk->vxkz") - mult(s_im, sin_tab, "vxyz,yk->vxkz")).astype(bf)
    h_im = (mult(s_im, cos_tab, "vxyz,yk->vxkz") + mult(s_re, sin_tab, "vxyz,yk->vxkz")).astype(bf)
    final = mult(h_re, cos_tab, "vxyz,zk->vxyk") - mult(h_im, sin_tab, "vxyz,zk->vxyk")
    potential = (final / float(NG**3)).astype(bf).reshape(col_local, planes * NG * NG)
    pot_rows = lax.all_to_all(potential, "vec", split_axis=1, concat_axis=0, tiled=True)
    return project(pair, pot_rows)


def solution(mesh):
    in_specs = (P(("grid", "vec"), None), P(), P())
    out_specs = P(("grid", "vec"), None)
    return jax.shard_map(shards, mesh=mesh, in_specs=in_specs, out_specs=out_specs, check_vma=False)
```

profile of v0, /device:TPU:0, one launch (start us, length us, event | category | flops | bytes accessed | tf_op | source)
XLA Modules:
  0.0 432.3 jit_solution(10535705733758545811)
XLA Ops:
  0.0 0.0 copy-start
  0.0 0.7 compare_and_fusion.1
  0.8 0.7 fusion.72
  1.5 20.8 %gather_fusion = bf16[2048,512]{1,0:T(8,128)(2,1)S(1)} fusion(bf16[27648,512]{1,0:T(8,128)(2,1)} %param.5, s32[2048]{0:T(1024)S(1)} %fusion.72), kind=kCustom, calls=%fused_computation | custom fusion | bytes 4202496 | tf_op jit(solution)/shard_map/jit(_take)/gather | solution.py:215
  22.3 0.9 select_select_fusion.refs_0_
  23.2 27.8 %exchange_total.3 = bf16[512,512]{1,0:T(8,128)(2,1)S(1)} custom-call(bf16[4,512,512]{2,1,0:T(8,128)(2,1)S(1)} %select_select_fusion.refs_0_), custom_call_target="tpu_custom_call" | custom-call | tf_op jit(solution)/shard_map/exchange_total/pallas_call | solution.py:125
  51.1 12.8 %exchange_total.4.refs_0_ = bf16[64,512]{1,0:T(8,128)(2,1)S(1)} custom-call(bf16[8,64,512]{2,1,0:T(8,128)(2,1)S(1)} %bitcast.110), custom_call_target="tpu_custom_call" | custom-call | tf_op jit(solution)/shard_map/exchange_total/pallas_call | solution.py:125
  63.9 14.9 %exchange_gather.2 = bf16[8,64,512]{2,1,0:T(8,128)(2,1)S(1)} custom-call(bf16[64,512]{1,0:T(8,128)(2,1)S(1)} %exchange_total.4.refs_0_), custom_call_target="tpu_custom_call" | custom-call | tf_op jit(solution)/shard_map/exchange_gather/pallas_call | solution.py:125
  78.8 26.9 %exchange_gather.3 = bf16[4,512,512]{2,1,0:T(8,128)(2,1)S(1)} custom-call(bf16[512,512]{1,0:T(8,128)(2,1)S(1)} %bitcast.111), custom_call_target="tpu_custom_call" | custom-call | tf_op jit(solution)/shard_map/exchange_gather/pallas_call | solution.py:125
  105.7 86.1 %while.10 = (s32[]{:T(128)}, bf16[4,6912,2048]{2,1,0:T(8,128)(2,1)}, bf16[4,6912,512]{2,1,0:T(8,128)(2,1)}, bf16[2048,512]{1,0:T(8,128)(2,1)S(1)}, s32[]{:T(128)}) while((s32[]{:T(128)}, bf16[4,6912,2048]{2,1,0:T(8,128)(2,1)}, bf16[4,6912,512]{2,1,0:T(8,128)(2,1)}, bf16[2048,512]{1,0:T(8,128)(2,1)S(1)}, s32[]{:T(128)}) %tuple.23), condition=%wide.region_1.2_spmd, body=%wide.region_0.1_spmd.sunk | while | flops 14523826176 | bytes 37487676 | solution.py:225
  105.7 21.5 %bitcast_dynamic-update-slice_fusion.2 = bf16[4,6912,2048]{2,1,0:T(8,128)(2,1)} fusion(bf16[4,6912,2048]{2,1,0:T(8,128)(2,1)} %get-tuple-element.69, s32[]{:T(128)} %get-tuple-element.68, bf16[2048,512]{1,0:T(8,128)(2,1)S(1)} %get-tuple-element.76, bf16[4,6912,512]{2,1,0:T(8,128)(2,1)} %get-tuple-element.75), kind=kOutput, calls=%fused_computation.2.clone.1 | convolution fusion | flops 14523826176 | bytes 37487616 | tf_op jit(solution)/shard_map/while/body/eval_jaxpr/dot_general | solution.py:220
  127.2 21.4 %bitcast_dynamic-update-slice_fusion.2 = bf16[4,6912,2048]{2,1,0:T(8,128)(2,1)} fusion(bf16[4,6912,2048]{2,1,0:T(8,128)(2,1)} %get-tuple-element.69, s32[]{:T(128)} %get-tuple-element.68, bf16[2048,512]{1,0:T(8,128)(2,1)S(1)} %get-tuple-element.76, bf16[4,6912,512]{2,1,0:T(8,128)(2,1)} %get-tuple-element.75), kind=kOutput, calls=%fused_computation.2.clone.1 | convolution fusion | flops 14523826176 | bytes 37487616 | tf_op jit(solution)/shard_map/while/body/eval_jaxpr/dot_general | solution.py:220
  148.7 21.5 %bitcast_dynamic-update-slice_fusion.2 = bf16[4,6912,2048]{2,1,0:T(8,128)(2,1)} fusion(bf16[4,6912,2048]{2,1,0:T(8,128)(2,1)} %get-tuple-element.69, s32[]{:T(128)} %get-tuple-element.68, bf16[2048,512]{1,0:T(8,128)(2,1)S(1)} %get-tuple-element.76, bf16[4,6912,512]{2,1,0:T(8,128)(2,1)} %get-tuple-element.75), kind=kOutput, calls=%fused_computation.2.clone.1 | convolution fusion | flops 14523826176 | bytes 37487616 | tf_op jit(solution)/shard_map/while/body/eval_jaxpr/dot_general | solution.py:220
  170.2 21.6 %bitcast_dynamic-update-slice_fusion.2 = bf16[4,6912,2048]{2,1,0:T(8,128)(2,1)} fusion(bf16[4,6912,2048]{2,1,0:T(8,128)(2,1)} %get-tuple-element.69, s32[]{:T(128)} %get-tuple-element.68, bf16[2048,512]{1,0:T(8,128)(2,1)S(1)} %get-tuple-element.76, bf16[4,6912,512]{2,1,0:T(8,128)(2,1)} %get-tuple-element.75), kind=kOutput, calls=%fused_computation.2.clone.1 | convolution fusion | flops 14523826176 | bytes 37487616 | tf_op jit(solution)/shard_map/while/body/eval_jaxpr/dot_general | solution.py:220
  191.8 0.0 copy-done
  191.8 42.6 %fusion.39 = bf16[4,8,216,128]{3,1,2,0:T(8,128)(2,1)S(1)} fusion(bf16[27648,2048]{1,0:T(8,128)(2,1)} %bitcast.7, bf16[2048,32]{0,1:T(8,128)(2,1)S(1)} %copy-done), kind=kOutput, calls=%fused_computation.48 | convolution fusion | flops 3624763392 | bytes 115146752 | tf_op jit(solution)/shard_map/dot_general | solution.py:228
  234.5 0.2 copy.88
  234.7 36.7 %exchange_blocks.2 = bf16[32,216,128]{2,1,0:T(8,128)(2,1)S(1)} custom-call(bf16[32,216,128]{2,1,0:T(8,128)(2,1)S(1)} %bitcast.109), custom_call_target="tpu_custom_call" | custom-call | tf_op jit(solution)/shard_map/exchange_blocks/pallas_call | solution.py:125
  271.4 3.0 reshape.223
  274.4 2.6 negate_convert_fusion
  277.0 0.0 copy-start.4
  277.0 1.0 fusion.51
  278.0 0.6 copy-done.4
  278.7 0.9 convolution_convert_fusion.1
  279.6 1.0 fusion.6
  280.6 1.2 fusion.27
  281.8 1.0 fusion.55
  282.9 1.0 fusion.5
  283.9 0.1 broadcast_add_fusion
  284.0 4.6 %multiply_convert_fusion.2 = bf16[96,96,96]{2,0,1:T(8,128)(2,1)S(1)} fusion(f32[96,96,96]{2,0,1:T(8,128)S(1)} %fusion.27, f32[96]{0:T(128)S(1)} %fusion.74, f32[96,96]{0,1:T(8,128)S(1)} %broadcast_add_fusion, bf16[96,96,96]{2,1,0:T(8,128)(2,1)S(1)} %fusion.5), kind=kOutput, calls=%fused_computation.16 | convolution fusion | flops 177039360 | bytes 7115136 | tf_op jit(solution)/shard_map/vxyz,xk->vkyz/dot_general | solution.py:38
  288.6 1.0 fusion.48
  289.6 1.2 fusion.31
  290.8 4.8 %multiply_convert_fusion.3 = bf16[96,96,96]{2,0,1:T(8,128)(2,1)S(1)} fusion(f32[96,96,96]{2,0,1:T(8,128)S(1)} %fusion.31, f32[96]{0:T(128)S(1)} %fusion.74, f32[96,96]{0,1:T(8,128)S(1)} %broadcast_add_fusion, bf16[96,96,96]{2,1,0:T(8,128)(2,1)S(1)} %fusion.6), kind=kOutput, calls=%fused_computation.17 | convolution fusion | flops 177039360 | bytes 7115136 | tf_op jit(solution)/shard_map/vxyz,xk->vkyz/dot_general | solution.py:38
  295.5 1.0 subtract_convert_fusion.1
  296.6 0.0 copy-start.3
  296.6 3.3 fusion.19
  299.9 0.0 copy-done.3
  299.9 1.0 fusion.58
  300.9 1.0 add_convert_fusion.1
  301.9 3.4 fusion.25
  305.3 7.4 %fusion.8 = f32[96,96,96]{2,1,0:T(8,128)} fusion(f32[96,96,96]{2,0,1:T(8,128)} %fusion.25, bf16[96,96,96]{2,0,1:T(8,128)(2,1)} %copy-done.3), kind=kOutput, calls=%fused_computation.24 | convolution fusion | flops 342577152 | bytes 8847360 | tf_op jit(solution)/shard_map/vxyz,zk->vxyk/dot_general | solution.py:38
  312.7 7.7 %multiply_convert_fusion.1 = bf16[96,96,96]{2,1,0:T(8,128)(2,1)} fusion(f32[96,96,96]{2,1,0:T(8,128)} %fusion.8, f32[96,96,96]{2,0,1:T(8,128)} %fusion.19, bf16[96,96,96]{2,0,1:T(8,128)(2,1)S(1)} %add_convert_fusion.1), kind=kOutput, calls=%fused_computation.11 | convolution fusion | flops 345231360 | bytes 10616832 | tf_op jit(solution)/shard_map/vxyz,zk->vxyk/dot_general | solution.py:38
  320.5 6.0 %reshape.228.refs_0_ = bf16[32,216,128]{2,1,0:T(8,128)(2,1)} reshape(bf16[96,96,96]{2,1,0:T(8,128)(2,1)} %multiply_convert_fusion.1) | data formatting | bytes 3538944 | tf_op jit(solution)/shard_map/reshape | solution.py:186
  326.5 0.0 copy-start.2
  326.5 1.5 copy-done.2
  327.9 44.2 %exchange_blocks.3 = bf16[32,216,128]{2,1,0:T(8,128)(2,1)S(1)} custom-call(bf16[32,216,128]{2,1,0:T(8,128)(2,1)S(1)} %copy-done.2), custom_call_target="tpu_custom_call" | custom-call | tf_op jit(solution)/shard_map/exchange_blocks/pallas_call | solution.py:125
  372.2 0.0 copy-start.1
  372.2 38.0 %convolution_multiply_fusion = f32[2048,32]{0,1:T(8,128)S(1)} fusion(bf16[27648,2048]{1,0:T(8,128)(2,1)} %bitcast.7, bf16[4,8,216,128]{3,2,1,0:T(8,128)(2,1)S(1)} %bitcast.108), kind=kOutput, calls=%fused_computation.31 | convolution fusion | flops 3623944192 | bytes 115277824 | tf_op jit(solution)/shard_map/dot_general | solution.py:192
  410.2 0.3 copy.54
  410.6 0.3 reshape.230.refs_0_
  410.9 20.4 %exchange_total.5 = f32[16,128]{1,0:T(8,128)S(1)} custom-call(f32[32,16,128]{2,1,0:T(8,128)S(1)} %reshape.230.refs_0_), custom_call_target="tpu_custom_call" | custom-call | tf_op jit(solution)/shard_map/exchange_total/pallas_call | solution.py:125
  431.2 0.1 reshape.231
  431.3 0.7 copy.55
  432.0 0.0 copy-done.1
  (4 shorter events, 0.0 us)
Async XLA Ops:
  0.0 191.8 %copy-start = (bf16[2048,32]{0,1:T(8,128)(2,1)S(1)}, bf16[2048,32]{0,1:T(8,128)(2,1)}, u32[]{:S(2)}) copy-start(bf16[2048,32]{0,1:T(8,128)(2,1)} %param.6) | copy-start | bytes 393220
  277.0 1.7 copy-start.4
  296.6 3.3 copy-start.3
  326.5 1.5 copy-start.2
  372.2 59.8 %copy-start.1 = (bf16[2048,32]{0,1:T(8,128)(2,1)S(1)}, bf16[2048,32]{0,1:T(8,128)(2,1)}, u32[]{:S(2)}) copy-start(bf16[2048,32]{0,1:T(8,128)(2,1)} %param.6) | copy-start | bytes 393220
where the time goes:
time: 437 us; the launch traced here: 432 us
  matrix products  212 us (49%)
  Pallas kernels  184 us (42%)
  local copies, waits for them, and re-layouts  33.5 us (8%)
    pallas_call x7, Pallas kernels, exchange(): pl.pallas_call(body, out_shape=jax.ShapeDtypeStruct(shape, blocks.dtype),...  184 us
    dot_general x4, matrix products, pair_block(): lax.dot_general(block, point_rows, (((1,), (1,)), ((), ())), preferred_el...  86.1 us
    dot_general x18, matrix products, mult(): return jnp.einsum(form, data, table, preferred_element_type=jnp.float32)  45.3 us
    dot_general x1, matrix products, shards(): lax.dot_general(inverse_panel, pair, (((0,), (1,)), ((), ())), preferred_...  42.6 us
    dot_general x1, matrix products, project(): lax.dot_general(pair, pot_rows, (((0,), (1,)), ((), ())), preferred_eleme...  38 us
    gather x1, local copies, waits for them, and re-layouts, shards(): picked = jnp.take(orbitals, jnp.clip(local_pos, 0, row_count - 1), axis=0)  20.8 us

commit v1 on v0

--- a/solution.py
+++ b/solution.py
@@ -157,36 +157,6 @@
     return exchange(block, 7, axes=("vec",), gather=True).reshape(npoints, norb)
 
 
-def transform(re, im, cos_tab, sin_tab, form, sign):
-    out_re = mult(re, cos_tab, form) + sign * mult(im, sin_tab, form)
-    out_im = mult(im, cos_tab, form) - sign * mult(re, sin_tab, form)
-    return out_re, out_im
-
-
-def solve_columns(fit_cols):
-    bf = jnp.bfloat16
-    count = fit_cols.shape[0]
-    rows = fit_cols.shape[1]
-    flat = exchange(fit_cols.reshape(count, rows // LANES, LANES), 1)
-    field = flat.reshape(1, NG, NG, NG)
-    cos_tab, sin_tab = wave_tables(NG)
-    waves = wavenumber(lax.iota(jnp.int32, NG), NG)
-    kernel = screened(waves, waves, waves)[None]
-    a_re = mult(field, cos_tab, "vxyz,zk->vxyk").astype(bf)
-    a_im = (-mult(field, sin_tab, "vxyz,zk->vxyk")).astype(bf)
-    b_re, b_im = transform(a_re, a_im, cos_tab, sin_tab, "vxyz,yk->vxkz", 1.0)
-    b_re, b_im = b_re.astype(bf), b_im.astype(bf)
-    h_re, h_im = transform(b_re, b_im, cos_tab, sin_tab, "vxyz,xk->vkyz", 1.0)
-    q_re, q_im = (h_re * kernel).astype(bf), (h_im * kernel).astype(bf)
-    g_re, g_im = transform(q_re, q_im, cos_tab, sin_tab, "vxyz,xk->vkyz", -1.0)
-    g_re, g_im = g_re.astype(bf), g_im.astype(bf)
-    p_re, p_im = transform(g_re, g_im, cos_tab, sin_tab, "vxyz,yk->vxkz", -1.0)
-    p_re, p_im = p_re.astype(bf), p_im.astype(bf)
-    final = mult(p_re, cos_tab, "vxyz,zk->vxyk") - mult(p_im, sin_tab, "vxyz,zk->vxyk")
-    potential = (final / float(NG**3)).astype(bf).reshape(flat.shape)
-    return exchange(potential, 2).reshape(count, rows)
-
-
 def project(pair, pot_rows):
     scale = 1.0 / math.sqrt(float(NG**3))
     term = lax.dot_general(
@@ -203,6 +173,479 @@
     return lax.psum_scatter(partial_block, "vec", scatter_dimension=0, tiled=True)
 
 
+def peers_of():
+    vec_count = lax.axis_size("vec")
+    count = lax.axis_size("grid") * vec_count
+    me = lax.axis_index("grid") * vec_count + lax.axis_index("vec")
+
+    def place(index):
+        return (index // vec_count, lax.rem(index, vec_count))
+
+    return count, me, place
+
+
+def greet_all(count, me, place):
+    barrier = pltpu.get_barrier_semaphore()
+
+    def greet(step, carry):
+        pl.semaphore_signal(
+            barrier,
+            inc=1,
+            device_id=place(lax.rem(me + step, count)),
+            device_id_type=pl.DeviceIdType.MESH,
+        )
+        return carry
+
+    lax.fori_loop(1, count, greet, 0)
+
+
+def wait_greeted(count):
+    pl.semaphore_wait(pltpu.get_barrier_semaphore(), count - 1)
+
+
+NT = (((1,), (1,)), ((), ()))
+NN = (((1,), (0,)), ((), ()))
+LINES = 16
+SPAN = LINES * NG
+TAKE = 512
+
+
+def pair_fit_kernel(
+    orb_ref, rows_ref, panel_ref, pair_ref, field_ref, fit_rows, out_buf, send_sem, recv_sem, own_sem
+):
+    bf = jnp.bfloat16
+    block = pl.program_id(0)
+    blocks = pl.num_programs(0)
+    count, me, place = peers_of()
+    npoints = rows_ref.shape[0]
+    cols = panel_ref.shape[0]
+    per_plane = NG // LINES
+
+    def target(index):
+        line = pl.multiple_of(lax.rem(index, per_plane) * LINES, LINES)
+        return field_ref.at[me, index // per_plane, pl.ds(line, LINES)]
+
+    def copy(index, step):
+        slot = lax.rem(index, 2)
+        peer = lax.rem(me + step, count)
+        return pltpu.make_async_remote_copy(
+            src_ref=out_buf.at[slot, peer],
+            dst_ref=target(index),
+            send_sem=send_sem.at[slot, step],
+            recv_sem=recv_sem.at[me],
+            device_id=place(peer),
+            device_id_type=pl.DeviceIdType.MESH,
+        )
+
+    def own(index):
+        slot = lax.rem(index, 2)
+        return pltpu.make_async_copy(out_buf.at[slot, me], target(index), own_sem.at[slot])
+
+    def send(index):
+        def body(step, carry):
+            copy(index, step).start()
+            return carry
+
+        own(index).start()
+        lax.fori_loop(1, count, body, 0)
+
+    def drain(index):
+        def body(step, carry):
+            copy(index, step).wait_send()
+            return carry
+
+        own(index).wait()
+        lax.fori_loop(1, count, body, 0)
+
+    @pl.when(block == 0)
+    def _():
+        greet_all(count, me, place)
+
+    @pl.when(block == 1)
+    def _():
+        wait_greeted(count)
+
+    @pl.when(block >= 1)
+    def _():
+        send(block - 1)
+
+    for first in range(0, npoints, TAKE):
+        part = lax.dot_general(
+            rows_ref[first : first + TAKE, :], orb_ref[...], NT, preferred_element_type=jnp.float32
+        )
+        pair_ref[0, first : first + TAKE, :] = (part * part).astype(bf)
+    fit = lax.dot_general(panel_ref[...], pair_ref[0], NN, preferred_element_type=jnp.float32)
+
+    for line in range(LINES):
+        begin = line * NG
+        low = begin // LANES * LANES
+        turn = begin - low
+        if low + 2 * LANES <= SPAN:
+            wide = fit[:, low : low + 2 * LANES]
+        else:
+            wide = jnp.concatenate([fit[:, low : low + LANES]] * 2, axis=1)
+        if turn:
+            wide = pltpu.roll(wide, 2 * LANES - turn, 1)
+        fit_rows[pl.ds(line, cols, stride=LINES), :] = wide[:, :LANES]
+
+    @pl.when(block >= 2)
+    def _():
+        drain(block - 2)
+
+    out_buf[lax.rem(block, 2)] = fit_rows[...].astype(bf).reshape(cols, LINES, LANES)
+
+    @pl.when(block == blocks - 1)
+    def _():
+        send(block)
+
+        def receive(step, carry):
+            source = lax.rem(me + count - step, count)
+            land = field_ref.at[source]
+            pltpu.make_async_copy(land, land, recv_sem.at[source]).wait()
+            return carry
+
+        lax.fori_loop(1, count, receive, 0)
+        drain(block - 1)
+        drain(block)
+
+
+def pair_and_fit(orbitals, point_rows, panel):
+    bf = jnp.bfloat16
+    rows, norb = orbitals.shape
+    npoints = point_rows.shape[0]
+    cols = panel.shape[0]
+    blocks = rows // SPAN
+    planes = rows // (NG * NG)
+    count = lax.axis_size("grid") * lax.axis_size("vec")
+    return pl.pallas_call(
+        pair_fit_kernel,
+        grid=(blocks,),
+        in_specs=[
+            pl.BlockSpec((SPAN, norb), lambda i: (i, 0)),
+            pl.BlockSpec((npoints, norb), lambda i: (0, 0)),
+            pl.BlockSpec((cols, npoints), lambda i: (0, 0)),
+        ],
+        out_specs=[
+            pl.BlockSpec((1, npoints, SPAN), lambda i: (i, 0, 0)),
+            pl.BlockSpec(memory_space=pl.ANY),
+        ],
+        out_shape=[
+            jax.ShapeDtypeStruct((blocks, npoints, SPAN), bf),
+            jax.ShapeDtypeStruct((count, planes, NG, LANES), bf),
+        ],
+        scratch_shapes=[
+            pltpu.VMEM((cols * LINES, LANES), jnp.float32),
+            pltpu.VMEM((2, cols, LINES, LANES), bf),
+            pltpu.SemaphoreType.DMA((2, count)),
+            pltpu.SemaphoreType.DMA((count,)),
+            pltpu.SemaphoreType.DMA((2,)),
+        ],
+        compiler_params=pltpu.CompilerParams(
+            collective_id=1, has_side_effects=True, vmem_limit_bytes=50 << 20
+        ),
+        name="pair_fit_send",
+    )(orbitals, point_rows, panel)
+
+
+GROUP = 8
+HALF = 64
+PIECE = NG * NG // LANES // 3
+
+
+def solve_kernel(field_ref, tz_ref, ty_ref, tyi_ref, tzi_ref, out_ref, by_y, by_x, flat, dense):
+    bf = jnp.bfloat16
+    f32 = jnp.float32
+    lane = lax.broadcasted_iota(jnp.int32, (NG, LANES), 1)
+    row = lax.broadcasted_iota(jnp.int32, (NG, LANES), 0)
+    sign = jnp.where(lane < HALF, 1.0, -1.0).astype(f32)
+    wave_z = lax.rem(lane, HALF).astype(f32)
+    wave_x = jnp.where(row < NG // 2, row, row - NG).astype(f32)
+    plane_sq = wave_x * wave_x + wave_z * wave_z
+    factor = NG / (2.0 * math.pi) * (NG / (2.0 * math.pi))
+
+    def both(parts):
+        top = jnp.concatenate([part.astype(bf) for part in parts], axis=1)
+        turned = [(pltpu.roll(part, HALF, 1) * sign).astype(bf) for part in parts]
+        return jnp.concatenate([top, jnp.concatenate(turned, axis=1)], axis=0)
+
+    def cut(wide, k):
+        return wide[:, k * LANES : (k + 1) * LANES]
+
+    def forward(step, carry):
+        first = step * GROUP
+        data = field_ref[pl.ds(first, GROUP)].reshape(GROUP * NG, LANES)
+        a = lax.dot_general(data, tz_ref[...], NN, preferred_element_type=f32).astype(bf)
+        top = [a[k * NG : (k + 1) * NG, :LANES] for k in range(GROUP)]
+        low = [a[k * NG : (k + 1) * NG, LANES:] for k in range(GROUP)]
+        stack = jnp.concatenate(
+            [jnp.concatenate(top, axis=1), jnp.concatenate(low, axis=1)], axis=0
+        )
+        b = lax.dot_general(ty_ref[...], stack, NN, preferred_element_type=f32)
+        for k in range(GROUP):
+            by_y[pl.ds(first + k, NG, stride=NG), :] = cut(b, k)
+        return carry
+
+    lax.fori_loop(0, NG // GROUP, forward, 0)
+
+    def middle(step, carry):
+        first = step * GROUP
+        parts = [by_y[pl.ds((first + k) * NG, NG), :] for k in range(GROUP)]
+        h = lax.dot_general(ty_ref[...], both(parts), NN, preferred_element_type=f32)
+        scaled = []
+        for k in range(GROUP):
+            index = first + k
+            wave_y = jnp.where(index < NG // 2, index, index - NG).astype(f32)
+            squared = plane_sq + wave_y * wave_y
+            kernel = jnp.where(squared > 0.5, factor / (squared + SCREEN), 0.0)
+            scaled.append(cut(h, k) * kernel)
+        g = lax.dot_general(tyi_ref[...], both(scaled), NN, preferred_element_type=f32)
+        for k in range(GROUP):
+            by_x[pl.ds(first + k, NG, stride=NG), :] = cut(g, k)
+        return carry
+
+    lax.fori_loop(0, NG // GROUP, middle, 0)
+
+    planes = NG // out_ref.shape[0]
+    quarter = NG // 4
+
+    def backward(step, carry):
+        first = step * GROUP
+        parts = [by_x[pl.ds((first + k) * NG, NG), :] for k in range(GROUP)]
+        p = lax.dot_general(tyi_ref[...], both(parts), NN, preferred_element_type=f32).astype(bf)
+        rows = jnp.concatenate([cut(p, k) for k in range(GROUP)], axis=0)
+        final = lax.dot_general(rows, tzi_ref[...], NN, preferred_element_type=f32)
+        flat[...] = final * f32(1.0 / float(NG**3))
+        for k in range(GROUP):
+            y0, y1, y2, y3 = [
+                flat[pl.ds(k * NG + j, quarter, stride=4), :] for j in range(4)
+            ]
+            spot = lane[:quarter]
+            dense[pl.ds(0, quarter, stride=3), :] = jnp.where(
+                spot < 96, y0, pltpu.roll(y1, 96, 1)
+            )
+            dense[pl.ds(1, quarter, stride=3), :] = jnp.where(
+                spot < 64, pltpu.roll(y1, 96, 1), pltpu.roll(y2, 64, 1)
+            )
+            dense[pl.ds(2, quarter, stride=3), :] = jnp.where(
+                spot < 32, pltpu.roll(y2, 64, 1), pltpu.roll(y3, 32, 1)
+            )
+            index = first + k
+            for m in range(3):
+                out_ref[index // planes, lax.rem(index, planes) * 3 + m] = dense[
+                    m * PIECE : (m + 1) * PIECE, :
+                ].astype(bf)
+        return carry
+
+    lax.fori_loop(0, NG // GROUP, backward, 0)
+
+
+def solve_field(field, count):
+    bf = jnp.bfloat16
+    f32 = jnp.float32
+    cos_tab, sin_tab = wave_tables(NG)
+    keep = NG // 2 + 1
+
+    def wide(table):
+        return jnp.pad(table[:, :keep], ((0, LANES - NG), (0, HALF - keep)))
+
+    cz, sz = wide(cos_tab), wide(sin_tab)
+    tz = jnp.concatenate([cz, -sz, -sz, -cz], axis=1)
+    ty = jnp.concatenate([cos_tab, sin_tab], axis=1)
+    tyi = jnp.concatenate([cos_tab, -sin_tab], axis=1)
+    spot = lax.iota(jnp.int32, HALF)[:, None]
+    weight = jnp.where((spot == 0) | (spot == NG // 2), 1.0, 2.0).astype(bf)
+    tzi = jnp.concatenate([cz.T * weight, -(sz.T * weight)], axis=0)
+    pieces = NG // count * 3
+    return pl.pallas_call(
+        solve_kernel,
+        out_shape=jax.ShapeDtypeStruct((count, pieces, PIECE, LANES), bf),
+        in_specs=[pl.BlockSpec(memory_space=pltpu.VMEM)] * 5,
+        out_specs=pl.BlockSpec(memory_space=pltpu.VMEM),
+        scratch_shapes=[
+            pltpu.VMEM((NG * NG, LANES), f32),
+            pltpu.VMEM((NG * NG, LANES), f32),
+            pltpu.VMEM((GROUP * NG, LANES), f32),
+            pltpu.VMEM((3 * PIECE, LANES), f32),
+        ],
+        compiler_params=pltpu.CompilerParams(vmem_limit_bytes=40 << 20),
+        name="solve_field",
+    )(field.reshape(NG, NG, LANES), tz, ty, tyi, tzi)
+
+
+RING = 6
+
+
+def project_kernel(
+    pot_ref, pair_ref, o_ref, ring, land, wide, total, parts, held,
+    send_sem, recv_sem, own_sem, pair_sem, part_send, part_recv,
+):
+    bf = jnp.bfloat16
+    f32 = jnp.float32
+    count, me, place = peers_of()
+    blocks, npoints, _ = pair_ref.shape
+    pieces = pot_ref.shape[1]
+    cols = count
+    share = npoints // count
+    per_piece = blocks // pieces
+    strips = SPAN // LANES
+
+    def fetch(block):
+        slot = lax.rem(block, RING)
+        return pltpu.make_async_copy(pair_ref.at[block], ring.at[slot], pair_sem.at[slot])
+
+    def prime(block, carry):
+        fetch(block).start()
+        return carry
+
+    greet_all(count, me, place)
+    lax.fori_loop(0, RING, prime, 0)
+    wait_greeted(count)
+
+    def copy(piece, step):
+        peer = lax.rem(me + step, count)
+        return pltpu.make_async_remote_copy(
+            src_ref=pot_ref.at[peer, piece],
+            dst_ref=land.at[piece, me],
+            send_sem=send_sem.at[piece],
+            recv_sem=recv_sem.at[piece],
+            device_id=place(peer),
+            device_id_type=pl.DeviceIdType.MESH,
+        )
+
+    def own(piece):
+        return pltpu.make_async_copy(pot_ref.at[me, piece], land.at[piece, me], own_sem.at[piece])
+
+    def send_piece(piece, carry):
+        def body(step, inner):
+            copy(piece, step).start()
+            return inner
+
+        own(piece).start()
+        return lax.fori_loop(1, count, body, carry)
+
+    lax.fori_loop(0, pieces, send_piece, 0)
+    total[...] = jnp.zeros_like(total)
+
+    def work(piece, carry):
+        own(piece).wait()
+        others = land.at[piece, pl.ds(0, count - 1)]
+        pltpu.make_async_copy(others, others, recv_sem.at[piece]).wait()
+        wide[...] = land[piece].astype(f32).reshape(cols * PIECE, LANES)
+        for half in range(per_piece):
+            block = piece * per_piece + half
+            slot = lax.rem(block, RING)
+            fetch(block).wait()
+            lines = [
+                wide[pl.ds(half * strips + j, cols, stride=PIECE), :].astype(bf)
+                for j in range(strips)
+            ]
+            total[...] += lax.dot_general(
+                jnp.concatenate(lines, axis=1), ring[slot], NT, preferred_element_type=f32
+            )
+
+            @pl.when(block + RING < blocks)
+            def _():
+                fetch(block + RING).start()
+
+        return carry
+
+    lax.fori_loop(0, pieces, work, 0)
+
+    scale = f32(1.0 / math.sqrt(float(NG**3)))
+    low_lane = lax.broadcasted_iota(jnp.int32, (cols // 2, LANES), 1) < share
+    for k in range(npoints // LANES):
+        tile = total[:, k * LANES : (k + 1) * LANES] * scale
+        top, low = tile[: cols // 2], tile[cols // 2 :]
+        parts[2 * k] = jnp.where(low_lane, top, pltpu.roll(low, share, 1))
+        parts[2 * k + 1] = jnp.where(low_lane, pltpu.roll(top, share, 1), low)
+
+    def part_copy(step, source, slot):
+        peer = lax.rem(me + step, count)
+        return pltpu.make_async_remote_copy(
+            src_ref=parts.at[source],
+            dst_ref=held.at[slot],
+            send_sem=part_send.at[step],
+            recv_sem=part_recv.at[step],
+            device_id=place(peer),
+            device_id_type=pl.DeviceIdType.MESH,
+        )
+
+    def part_start(step, carry):
+        part_copy(step, lax.rem(me + step, count), me).start()
+        return carry
+
+    lax.fori_loop(1, count, part_start, 0)
+    held[me] = parts[me]
+
+    def drain_piece(piece, carry):
+        sent = pot_ref.at[pl.ds(0, count - 1), piece]
+        pltpu.make_async_copy(sent, sent, send_sem.at[piece]).wait()
+        return carry
+
+    lax.fori_loop(0, pieces, drain_piece, 0)
+
+    def part_receive(step, carry):
+        source = lax.rem(me + count - step, count)
+        part_copy(step, source, source).wait_recv()
+        return carry
+
+    lax.fori_loop(1, count, part_receive, 0)
+    summed = jnp.sum(held[...], axis=0)
+    both = jnp.concatenate([summed, pltpu.roll(summed, share, 1)], axis=0)
+    o_ref[...] = both.T[:share, :]
+
+    def part_drain(step, carry):
+        part_copy(step, lax.rem(me + step, count), me).wait_send()
+        return carry
+
+    lax.fori_loop(1, count, part_drain, 0)
+
+
+def send_and_project(potential, pair):
+    bf = jnp.bfloat16
+    f32 = jnp.float32
+    count, pieces = potential.shape[:2]
+    blocks, npoints, span = pair.shape
+    cols = count
+    share = npoints // count
+    return pl.pallas_call(
+        project_kernel,
+        out_shape=jax.ShapeDtypeStruct((share, cols), f32),
+        in_specs=[pl.BlockSpec(memory_space=pltpu.VMEM), pl.BlockSpec(memory_space=pl.ANY)],
+        out_specs=pl.BlockSpec(memory_space=pltpu.VMEM),
+        scratch_shapes=[
+            pltpu.VMEM((RING, npoints, span), bf),
+            pltpu.VMEM((pieces, count, PIECE, LANES), bf),
+            pltpu.VMEM((cols * PIECE, LANES), f32),
+            pltpu.VMEM((cols, npoints), f32),
+            pltpu.VMEM((count, cols // 2, LANES), f32),
+            pltpu.VMEM((count, cols // 2, LANES), f32),
+            pltpu.SemaphoreType.DMA((pieces,)),
+            pltpu.SemaphoreType.DMA((pieces,)),
+            pltpu.SemaphoreType.DMA((pieces,)),
+            pltpu.SemaphoreType.DMA((RING,)),
+            pltpu.SemaphoreType.DMA((count,)),
+            pltpu.SemaphoreType.DMA((count,)),
+        ],
+        compiler_params=pltpu.CompilerParams(
+            collective_id=2, has_side_effects=True, vmem_limit_bytes=54 << 20
+        ),
+        name="send_project",
+    )(potential, pair)
+
+
+def fits_planes(rows, npoints, cols, count):
+    blocks = rows // SPAN
+    return (
+        cols == count
+        and rows % (NG * NG) == 0
+        and NG % (rows // (NG * NG)) == 0
+        and blocks >= max(RING, 3)
+        and npoints % TAKE == 0
+        and 2 * npoints == count * LANES
+    )
+
+
 def shards(orbitals, inverse_panel, points):
     bf = jnp.bfloat16
     row_count = orbitals.shape[0]
@@ -216,6 +659,10 @@
     picked = jnp.where(inside[:, None], picked, jnp.zeros_like(picked))
     point_rows = share_rows(picked, grid_count, vec_count)
 
+    if fits_planes(row_count, npoints, inverse_panel.shape[1], grid_count * vec_count):
+        pair, field = pair_and_fit(orbitals, point_rows, inverse_panel.T)
+        return send_and_project(solve_field(field, grid_count * vec_count), pair)
+
     def pair_block(block):
         correlation = lax.dot_general(
             block, point_rows, (((1,), (1,)), ((), ())), preferred_element_type=jnp.float32
@@ -228,8 +675,6 @@
     fit_cols = lax.dot_general(
         inverse_panel, pair, (((0,), (1,)), ((), ())), preferred_element_type=jnp.float32
     ).astype(bf)
-    if inverse_panel.shape[1] == grid_count * vec_count and row_count % LANES == 0:
-        return project(pair, solve_columns(fit_cols))
     slab = lax.all_to_all(fit_cols, "vec", split_axis=0, concat_axis=1, tiled=True)
     col_local = slab.shape[0]
     planes = NG // grid_count

time: 437 us -> 309 us (0.71)
  matrix products: 212 us -> 0 us
  Pallas kernels: 184 us -> 280 us
  local copies, waits for them, and re-layouts: 33.5 us -> 25.1 us
    dot_general x24 -> x0, matrix products: 212 us -> none  [the longest x4 86.1 us: pair_block(): lax.dot_general(block, point_rows, (((1,), (1,)), ((), ())), preferred_el...]
    pallas_call x0 -> x3, Pallas kernels: none -> 198 us  [the longest x1 113 us: pair_and_fit(): pl.pallas_call(pair_fit_kernel, grid=(blocks,), in_specs=[pl.BlockSpec((S...]
    pallas_call x7 -> x4, Pallas kernels: 184 us -> 82.4 us  [exchange(): pl.pallas_call(body, out_shape=jax.ShapeDtypeStruct(shape, blocks.dtype),...]
    reshape x4 -> x0, local copies, waits for them, and re-layouts: 7.02 us -> none  [the longest x1 5.99 us: solve_columns(): potential = (final / float(NG ** 3)).astype(bf).reshape(flat.shape)]
where the time goes in v1:
time: 309 us; the launch traced here: 308 us
  Pallas kernels  280 us (91%)
  local copies, waits for them, and re-layouts  25.1 us (8%)
    pallas_call x1, Pallas kernels, pair_and_fit(): pl.pallas_call(pair_fit_kernel, grid=(blocks,), in_specs=[pl.BlockSpec((S...  113 us
    pallas_call x4, Pallas kernels, exchange(): pl.pallas_call(body, out_shape=jax.ShapeDtypeStruct(shape, blocks.dtype),...  82.4 us
    pallas_call x1, Pallas kernels, send_and_project(): pl.pallas_call(project_kernel, out_shape=jax.ShapeDtypeStruct((share, col...  61.8 us
    pallas_call x1, Pallas kernels, solve_field(): pl.pallas_call(solve_kernel, out_shape=jax.ShapeDtypeStruct((count, piece...  23 us
    gather x1, local copies, waits for them, and re-layouts, shards(): picked = jnp.take(orbitals, jnp.clip(local_pos, 0, row_count - 1), axis=0)  20.5 us

profile of v1, /device:TPU:0, one launch (start us, length us, event | category | flops | bytes accessed | tf_op | source)
XLA Modules:
  0.0 307.8 jit_solution(10839423710349891248)
XLA Ops:
  0.0 0.7 fusion.6
  0.7 0.0 copy-start.3
  0.7 20.5 %gather_fusion = bf16[2048,512]{1,0:T(8,128)(2,1)S(1)} fusion(bf16[27648,512]{1,0:T(8,128)(2,1)} %orb_ref.1, s32[2048]{0:T(1024)S(1)} %fusion.6), kind=kCustom, calls=%fused_computation | custom fusion | bytes 4202496 | tf_op jit(solution)/shard_map/jit(_take)/gather | solution.py:658
  21.2 0.0 copy-done.3
  21.2 0.9 select_select_fusion.refs_0_
  22.2 27.8 %exchange_total.2 = bf16[512,512]{1,0:T(8,128)(2,1)S(1)} custom-call(bf16[4,512,512]{2,1,0:T(8,128)(2,1)S(1)} %select_select_fusion.refs_0_), custom_call_target="tpu_custom_call" | custom-call | tf_op jit(solution)/shard_map/exchange_total/pallas_call | solution.py:125
  50.0 0.0 copy-start.2
  50.0 12.8 %exchange_total.3.refs_0_ = bf16[64,512]{1,0:T(8,128)(2,1)S(1)} custom-call(bf16[8,64,512]{2,1,0:T(8,128)(2,1)S(1)} %bitcast.12), custom_call_target="tpu_custom_call" | custom-call | tf_op jit(solution)/shard_map/exchange_total/pallas_call | solution.py:125
  62.8 14.9 %exchange_gather.2 = bf16[8,64,512]{2,1,0:T(8,128)(2,1)S(1)} custom-call(bf16[64,512]{1,0:T(8,128)(2,1)S(1)} %exchange_total.3.refs_0_), custom_call_target="tpu_custom_call" | custom-call | tf_op jit(solution)/shard_map/exchange_gather/pallas_call | solution.py:125
  77.7 26.9 %exchange_gather.3 = bf16[4,512,512]{2,1,0:T(8,128)(2,1)S(1)} custom-call(bf16[512,512]{1,0:T(8,128)(2,1)S(1)} %bitcast.13), custom_call_target="tpu_custom_call" | custom-call | tf_op jit(solution)/shard_map/exchange_gather/pallas_call | solution.py:125
  104.7 0.0 copy-done.2
  104.7 113.0 %pair_fit_send.1 = (bf16[18,2048,1536]{2,1,0:T(8,128)(2,1)}, bf16[32,3,96,128]{3,2,1,0:T(8,128)(2,1)}) custom-call(bf16[27648,512]{1,0:T(8,128)(2,1)} %orb_ref.1, bf16[2048,512]{1,0:T(8,128)(2,1)S(1)} %bitcast.10, bf16[32,2048]{1,0:T(8,128)(2,1)S(1)} %bitcast.14), custom_call_target="tpu_custom_call" | custom-call | tf_op jit(solution)/shard_map/pair_fit_send/pallas_call | solution.py:320
  217.7 0.2 sine_convert_fusion
  217.9 0.1 multiply_bitcast_fusion
  218.0 0.1 copy.4.tz_ref
  218.2 0.2 fusion.5
  218.4 0.1 copy.5.ty_ref
  218.5 0.1 copy.6.tyi_ref
  218.6 0.0 copy-start.1
  218.6 1.7 copy-done.1
  220.3 23.0 %solve_field.1.pot_ref = bf16[32,9,24,128]{3,2,1,0:T(8,128)(2,1)S(1)} custom-call(bf16[96,96,128]{2,1,0:T(8,128)(2,1)S(1)} %bitcast.11, bf16[128,256]{1,0:T(8,128)(2,1)S(1)} %copy.4.tz_ref, bf16[96,192]{1,0:T(8,128)(2,1)S(1)} %copy.5.ty_ref, bf16[96,192]{1,0:T(8,128)(2,1)S(1)} %copy.6.tyi_ref, bf16[128,128]{1,0:T(8,128)(2,1)S(1)} %pad_maximum_fusion.3.tzi_ref), custom_call_target="tpu_custom_call" | custom-call | tf_op jit(solution)/shard_map/solve_field/pallas_call | solution.py:459
  243.3 0.0 copy-start
  243.3 1.2 copy-done
  244.5 61.8 %send_project.1 = f32[64,32]{1,0:T(8,128)} custom-call(bf16[32,9,24,128]{3,2,1,0:T(8,128)(2,1)} %copy-done, bf16[18,2048,1536]{2,1,0:T(8,128)(2,1)} %get-tuple-element.8.pair_ref), custom_call_target="tpu_custom_call" | custom-call | tf_op jit(solution)/shard_map/send_project/pallas_call | solution.py:611
  306.3 1.4 copy.7
  (9 shorter events, 0.1 us)
Async XLA Ops:
  0.7 20.5 %copy-start.3 = (s32[2048]{0:T(1024)S(1)}, s32[2048]{0:T(1024)}, u32[]{:S(2)}) copy-start(s32[2048]{0:T(1024)} %param.5) | copy-start | bytes 24580
  50.0 54.7 %copy-start.2 = (bf16[2048,32]{0,1:T(8,128)(2,1)S(1)}, bf16[2048,32]{0,1:T(8,128)(2,1)}, u32[]{:S(2)}) copy-start(bf16[2048,32]{0,1:T(8,128)(2,1)} %param.4) | copy-start | bytes 393220
  218.6 1.7 copy-start.1
  243.3 1.2 copy-start

commit v2 on v1

--- a/solution.py
+++ b/solution.py
@@ -140,21 +140,239 @@
     )(blocks)
 
 
+def share_kernel(chunks, x_ref, o_ref, near, wide, far, sum1, sum2, sum3, sends, recvs, own_sem):
+    bf = jnp.bfloat16
+    f32 = jnp.float32
+    vec_count = lax.axis_size("vec")
+    deep = lax.axis_size("grid") // 2
+    grid_at, mine = lax.axis_index("grid"), lax.axis_index("vec")
+    level, core = grid_at // 2, lax.rem(grid_at, 2)
+    other = 1 - core
+    across = vec_count - 1
+
+    def partner(step):
+        return (level * 2 + other, mine)
+
+    def beside(step):
+        return (grid_at, lax.rem(mine + step, vec_count))
+
+    def above(step):
+        return (lax.rem(level + step, deep) * 2 + core, mine)
+
+    peers = [partner(1)]
+    peers += [beside(step) for step in range(1, vec_count)]
+    peers += [above(step) for step in range(1, deep)]
+    barrier = pltpu.get_barrier_semaphore()
+    for peer in peers:
+        pl.semaphore_signal(barrier, inc=1, device_id=peer, device_id_type=pl.DeviceIdType.MESH)
+    pl.semaphore_wait(barrier, len(peers))
+
+    def send(source, target, slot, peer):
+        return pltpu.make_async_remote_copy(
+            src_ref=source,
+            dst_ref=target,
+            send_sem=sends.at[slot],
+            recv_sem=recvs.at[slot],
+            device_id=peer,
+            device_id_type=pl.DeviceIdType.MESH,
+        )
+
+    per_chunk = 2 + 2 * across + 2 * (deep - 1)
+
+    def copies(stage, c):
+        base = c * per_chunk
+        if stage == 0:
+            return [send(x_ref.at[c, other], near.at[c], base, partner(1))]
+        if stage == 1:
+            return [
+                send(
+                    sum1.at[c, lax.rem(mine + step, vec_count)],
+                    wide.at[c, step - 1],
+                    base + step,
+                    beside(step),
+                )
+                for step in range(1, vec_count)
+            ]
+        if stage == 2:
+            return [
+                send(
+                    sum2.at[c, lax.rem(level + step, deep)],
+                    far.at[c, step - 1],
+                    base + across + step,
+                    above(step),
+                )
+                for step in range(1, deep)
+            ]
+        base += across + deep
+        if stage == 3:
+            spot = o_ref.at[c, core, mine, level]
+            return [send(sum3.at[c], spot, base + step - 1, above(step)) for step in range(1, deep)]
+        base += deep - 1
+        if stage == 4:
+            spot = o_ref.at[c, core, mine]
+            return [send(spot, spot, base + step - 1, beside(step)) for step in range(1, vec_count)]
+        spot = o_ref.at[c, core]
+        return [send(spot, spot, base + across, partner(1))]
+
+    def own(c):
+        return pltpu.make_async_copy(sum3.at[c], o_ref.at[c, core, mine, level], own_sem.at[c])
+
+    def prepare(stage, c):
+        for move in copies(stage - 1, c):
+            move.wait_recv()
+        if stage == 1:
+            sum1[c] = (x_ref[c, core].astype(f32) + near[c].astype(f32)).astype(bf)
+        if stage == 2:
+            total = sum1[c, mine].astype(f32)
+            for step in range(across):
+                total += wide[c, step].astype(f32)
+            sum2[c] = total.astype(bf)
+        if stage == 3:
+            total = sum2[c, level].astype(f32)
+            for step in range(deep - 1):
+                total += far[c, step].astype(f32)
+            sum3[c] = total.astype(bf)
+            own(c).start()
+        if stage == 4:
+            own(c).wait()
+
+    for tick in range(chunks + 6):
+        for stage in range(6, -1, -1):
+            c = tick - stage
+            if 0 <= c < chunks:
+                if stage > 0:
+                    prepare(stage, c)
+                if stage < 6:
+                    for move in copies(stage, c):
+                        move.start()
+    for c in range(chunks):
+        for stage in range(6):
+            for move in copies(stage, c):
+                move.wait_send()
+
+
+ROWS = 16
+
+
 def share_rows(picked, grid_count, vec_count):
+    bf = jnp.bfloat16
     npoints, norb = picked.shape
-    if npoints % (grid_count * vec_count * 16) != 0:
+    count = grid_count * vec_count
+    if npoints % (count * ROWS) != 0 or grid_count % 2 != 0:
         return lax.psum(picked.astype(jnp.float32), ("grid", "vec")).astype(picked.dtype)
-    mine = exchange(
-        picked.reshape(vec_count, npoints // vec_count, norb), 4, total=True, axes=("vec",)
-    )
-    mine = exchange(
-        mine.reshape(grid_count, npoints // vec_count // grid_count, norb),
-        5,
-        total=True,
-        axes=("grid",),
-    )
-    block = exchange(mine, 6, axes=("grid",), gather=True).reshape(npoints // vec_count, norb)
-    return exchange(block, 7, axes=("vec",), gather=True).reshape(npoints, norb)
+    chunks = npoints // (count * ROWS)
+    deep = grid_count // 2
+    shape = (chunks, 2, vec_count, deep, ROWS, norb)
+    slots = chunks * (2 + 2 * (vec_count - 1) + 2 * (deep - 1))
+
+    def body(*refs):
+        share_kernel(chunks, *refs)
+
+    return pl.pallas_call(
+        body,
+        out_shape=jax.ShapeDtypeStruct(shape, bf),
+        in_specs=[pl.BlockSpec(memory_space=pltpu.VMEM)],
+        out_specs=pl.BlockSpec(memory_space=pltpu.VMEM),
+        scratch_shapes=[
+            pltpu.VMEM((chunks, vec_count, deep, ROWS, norb), bf),
+            pltpu.VMEM((chunks, vec_count - 1, deep, ROWS, norb), bf),
+            pltpu.VMEM((chunks, deep - 1, ROWS, norb), bf),
+            pltpu.VMEM((chunks, vec_count, deep, ROWS, norb), bf),
+            pltpu.VMEM((chunks, deep, ROWS, norb), bf),
+            pltpu.VMEM((chunks, ROWS, norb), bf),
+            pltpu.SemaphoreType.DMA((slots,)),
+            pltpu.SemaphoreType.DMA((slots,)),
+            pltpu.SemaphoreType.DMA((chunks,)),
+        ],
+        compiler_params=pltpu.CompilerParams(
+            collective_id=4, has_side_effects=True, vmem_limit_bytes=32 << 20
+        ),
+        name="share_rows",
+    )(picked.reshape(shape)).reshape(npoints, norb)
+
+
+OCTET = 8
+
+
+def pick_kernel(points_ref, flags_ref, offset_ref, orb_ref, o_ref, found, where, spare, sheet, sem):
+    octets, _, norb = orb_ref.shape
+    limit = octets * OCTET
+    npoints = o_ref.shape[0]
+    offset = offset_ref[0]
+    sheet[...] = jnp.zeros_like(sheet)
+
+    def fetch(slot, octet):
+        return pltpu.make_async_copy(orb_ref.at[octet], found.at[slot], sem)
+
+    def look(i, held):
+        position = points_ref[i] - offset
+        inside = (position >= 0) & (position < limit)
+
+        @pl.when(inside)
+        def _():
+            fetch(held, position // OCTET).start()
+            where[held] = i
+            spare[held] = lax.rem(position, OCTET)
+
+        return held + inside.astype(jnp.int32)
+
+    def scan(group, held):
+        return lax.cond(
+            flags_ref[group] > 0,
+            lambda h: lax.fori_loop(0, OCTET, lambda k, n: look(group * OCTET + k, n), h),
+            lambda h: h,
+            held,
+        )
+
+    held = lax.fori_loop(0, npoints // OCTET, scan, 0)
+
+    def settle(slot, carry):
+        fetch(slot, 0).wait()
+        return carry
+
+    lax.fori_loop(0, held, settle, 0)
+    line = lax.broadcasted_iota(jnp.int32, (OCTET, norb), 0)
+
+    def place(slot, carry):
+        octet = found[slot].astype(jnp.float32)
+        row = jnp.sum(jnp.where(line == spare[slot], octet, 0.0), axis=0, keepdims=True)
+        sheet[pl.ds(where[slot], 1), :] = row
+        return carry
+
+    lax.fori_loop(0, held, place, 0)
+    o_ref[...] = sheet[...].astype(o_ref.dtype)
+
+
+def pick_rows(orbitals, points, offset):
+    rows, norb = orbitals.shape
+    npoints = points.shape[0]
+    position = points - offset
+    if rows % OCTET != 0 or npoints % OCTET != 0:
+        inside = (position >= 0) & (position < rows)
+        picked = jnp.take(orbitals, jnp.clip(position, 0, rows - 1), axis=0)
+        return jnp.where(inside[:, None], picked, jnp.zeros_like(picked))
+    inside = (position >= 0) & (position < rows)
+    flags = jnp.max(inside.reshape(-1, OCTET).astype(jnp.int32), axis=1)
+    return pl.pallas_call(
+        pick_kernel,
+        out_shape=jax.ShapeDtypeStruct((npoints, norb), orbitals.dtype),
+        in_specs=[
+            pl.BlockSpec(memory_space=pltpu.SMEM),
+            pl.BlockSpec(memory_space=pltpu.SMEM),
+            pl.BlockSpec(memory_space=pltpu.SMEM),
+            pl.BlockSpec(memory_space=pl.ANY),
+        ],
+        out_specs=pl.BlockSpec(memory_space=pltpu.VMEM),
+        scratch_shapes=[
+            pltpu.VMEM((npoints, OCTET, norb), orbitals.dtype),
+            pltpu.SMEM((npoints,), jnp.int32),
+            pltpu.SMEM((npoints,), jnp.int32),
+            pltpu.VMEM((npoints, norb), jnp.float32),
+            pltpu.SemaphoreType.DMA(()),
+        ],
+        compiler_params=pltpu.CompilerParams(vmem_limit_bytes=40 << 20),
+        name="pick_rows",
+    )(points, flags, offset[None].astype(jnp.int32), orbitals.reshape(rows // OCTET, OCTET, norb))
 
 
 def project(pair, pot_rows):
@@ -208,10 +426,12 @@
 LINES = 16
 SPAN = LINES * NG
 TAKE = 512
+JOIN = 3
 
 
 def pair_fit_kernel(
-    orb_ref, rows_ref, panel_ref, pair_ref, field_ref, fit_rows, out_buf, send_sem, recv_sem, own_sem
+    orb_ref, rows_ref, panel_ref, pair_ref, field_ref, fit_buf, fit_rows, out_buf,
+    send_sem, recv_sem, own_sem,
 ):
     bf = jnp.bfloat16
     block = pl.program_id(0)
@@ -220,42 +440,37 @@
     npoints = rows_ref.shape[0]
     cols = panel_ref.shape[0]
     per_plane = NG // LINES
-
-    def target(index):
-        line = pl.multiple_of(lax.rem(index, per_plane) * LINES, LINES)
-        return field_ref.at[me, index // per_plane, pl.ds(line, LINES)]
-
-    def copy(index, step):
-        slot = lax.rem(index, 2)
-        peer = lax.rem(me + step, count)
-        return pltpu.make_async_remote_copy(
-            src_ref=out_buf.at[slot, peer],
-            dst_ref=target(index),
-            send_sem=send_sem.at[slot, step],
-            recv_sem=recv_sem.at[me],
-            device_id=place(peer),
-            device_id_type=pl.DeviceIdType.MESH,
-        )
-
-    def own(index):
-        slot = lax.rem(index, 2)
-        return pltpu.make_async_copy(out_buf.at[slot, me], target(index), own_sem.at[slot])
-
-    def send(index):
+    groups = blocks // JOIN
+    tall = JOIN * LINES
+
+    def send(group, begin, lines):
+        slot = lax.rem(group, 2)
+        start = pl.multiple_of(lax.rem(group * JOIN, per_plane) * LINES + begin, LINES)
+        target = field_ref.at[me, group * JOIN // per_plane, pl.ds(start, lines)]
+
         def body(step, carry):
-            copy(index, step).start()
+            peer = lax.rem(me + step, count)
+            pltpu.make_async_remote_copy(
+                src_ref=out_buf.at[slot, peer, pl.ds(begin, lines)],
+                dst_ref=target,
+                send_sem=send_sem.at[slot],
+                recv_sem=recv_sem.at[me],
+                device_id=place(peer),
+                device_id_type=pl.DeviceIdType.MESH,
+            ).start()
             return carry
 
-        own(index).start()
-        lax.fori_loop(1, count, body, 0)
-
-    def drain(index):
-        def body(step, carry):
-            copy(index, step).wait_send()
-            return carry
-
-        own(index).wait()
-        lax.fori_loop(1, count, body, 0)
+        pltpu.make_async_copy(
+            out_buf.at[slot, me, pl.ds(begin, lines)], target, own_sem.at[slot]
+        ).start()
+        lax.fori_loop(1, count, body, 0, unroll=True)
+
+    def drain(group):
+        slot = lax.rem(group, 2)
+        sent = out_buf.at[slot, pl.ds(0, count - 1)]
+        mine = out_buf.at[slot, me]
+        pltpu.make_async_copy(mine, mine, own_sem.at[slot]).wait()
+        pltpu.make_async_copy(sent, sent, send_sem.at[slot]).wait()
 
     @pl.when(block == 0)
     def _():
@@ -265,38 +480,64 @@
     def _():
         wait_greeted(count)
 
-    @pl.when(block >= 1)
+    before = jnp.maximum(block - 1, 0)
+
+    @pl.when((block > 2 * JOIN) & (lax.rem(before, JOIN) == 0))
     def _():
-        send(block - 1)
-
-    for first in range(0, npoints, TAKE):
+        drain(before // JOIN - 2)
+
+    def multiply(first):
         part = lax.dot_general(
             rows_ref[first : first + TAKE, :], orb_ref[...], NT, preferred_element_type=jnp.float32
         )
         pair_ref[0, first : first + TAKE, :] = (part * part).astype(bf)
-    fit = lax.dot_general(panel_ref[...], pair_ref[0], NN, preferred_element_type=jnp.float32)
-
-    for line in range(LINES):
-        begin = line * NG
-        low = begin // LANES * LANES
-        turn = begin - low
-        if low + 2 * LANES <= SPAN:
-            wide = fit[:, low : low + 2 * LANES]
-        else:
-            wide = jnp.concatenate([fit[:, low : low + LANES]] * 2, axis=1)
-        if turn:
-            wide = pltpu.roll(wide, 2 * LANES - turn, 1)
-        fit_rows[pl.ds(line, cols, stride=LINES), :] = wide[:, :LANES]
-
-    @pl.when(block >= 2)
+
+    def arrange(index):
+        for line in range(LINES):
+            begin = line * NG
+            low = begin // LANES * LANES
+            turn = begin - low
+            wide = fit_buf[:, low : min(low + 2 * LANES, SPAN)]
+            if wide.shape[1] == LANES:
+                wide = jnp.concatenate([wide, wide], axis=1)
+            if turn:
+                wide = pltpu.roll(wide, 2 * LANES - turn, 1)
+            fit_rows[pl.ds(line, cols, stride=LINES), :] = wide[:, :LANES]
+        slot = lax.rem(index // JOIN, 2)
+        begin = pl.multiple_of(lax.rem(index, JOIN) * LINES, LINES)
+        out_buf[slot, :, pl.ds(begin, LINES), :] = (
+            fit_rows[...].astype(bf).reshape(cols, LINES, LANES)
+        )
+
+    @pl.when(block == 0)
     def _():
-        drain(block - 2)
-
-    out_buf[lax.rem(block, 2)] = fit_rows[...].astype(bf).reshape(cols, LINES, LANES)
+        fit_buf[...] = jnp.zeros_like(fit_buf)
+
+    multiply(0)
+    arrange(before)
+    for first in range(TAKE, npoints // 2, TAKE):
+        multiply(first)
+
+    @pl.when((block >= JOIN) & (lax.rem(block, JOIN) == 0))
+    def _():
+        send(block // JOIN - 1, 0, tall)
+
+    for late in range(JOIN - 1):
+
+        @pl.when(block == blocks - JOIN + 1 + late)
+        def _(late=late):
+            send(groups - 1, late * LINES, LINES)
+
+    for first in range(npoints // 2, npoints, TAKE):
+        multiply(first)
+    fit_buf[...] = lax.dot_general(
+        panel_ref[...], pair_ref[0], NN, preferred_element_type=jnp.float32
+    )
 
     @pl.when(block == blocks - 1)
     def _():
-        send(block)
+        arrange(block)
+        send(groups - 1, (JOIN - 1) * LINES, LINES)
 
         def receive(step, carry):
             source = lax.rem(me + count - step, count)
@@ -305,8 +546,8 @@
             return carry
 
         lax.fori_loop(1, count, receive, 0)
-        drain(block - 1)
-        drain(block)
+        drain(groups - 2)
+        drain(groups - 1)
 
 
 def pair_and_fit(orbitals, point_rows, panel):
@@ -334,9 +575,10 @@
             jax.ShapeDtypeStruct((count, planes, NG, LANES), bf),
         ],
         scratch_shapes=[
+            pltpu.VMEM((cols, SPAN), jnp.float32),
             pltpu.VMEM((cols * LINES, LANES), jnp.float32),
-            pltpu.VMEM((2, cols, LINES, LANES), bf),
-            pltpu.SemaphoreType.DMA((2, count)),
+            pltpu.VMEM((2, cols, JOIN * LINES, LANES), bf),
+            pltpu.SemaphoreType.DMA((2,)),
             pltpu.SemaphoreType.DMA((count,)),
             pltpu.SemaphoreType.DMA((2,)),
         ],
@@ -640,7 +882,8 @@
         cols == count
         and rows % (NG * NG) == 0
         and NG % (rows // (NG * NG)) == 0
-        and blocks >= max(RING, 3)
+        and blocks >= max(RING, 2 * JOIN)
+        and NG // LINES % JOIN == 0
         and npoints % TAKE == 0
         and 2 * npoints == count * LANES
     )
@@ -653,10 +896,7 @@
     vec_count = lax.axis_size("vec")
     npoints = points.shape[0]
     offset = (lax.axis_index("grid") * vec_count + lax.axis_index("vec")) * row_count
-    local_pos = points - offset
-    inside = (local_pos >= 0) & (local_pos < row_count)
-    picked = jnp.take(orbitals, jnp.clip(local_pos, 0, row_count - 1), axis=0)
-    picked = jnp.where(inside[:, None], picked, jnp.zeros_like(picked))
+    picked = pick_rows(orbitals, points, offset)
     point_rows = share_rows(picked, grid_count, vec_count)
 
     if fits_planes(row_count, npoints, inverse_panel.shape[1], grid_count * vec_count):

time: 309 us -> 248 us (0.80)
  Pallas kernels: 280 us -> 240 us
  local copies, waits for them, and re-layouts: 25.1 us -> 5.41 us
    pallas_call x4 -> x2, Pallas kernels: 82.4 us -> 55.2 us  [the longest x1 43.5 us: share_rows(): pl.pallas_call(body, out_shape=jax.ShapeDtypeStruct(shape, bf), in_specs=...]
    gather x1 -> x0, local copies, waits for them, and re-layouts: 20.5 us -> none  [shards(): picked = jnp.take(orbitals, jnp.clip(local_pos, 0, row_count - 1), axis=0)]
    pallas_call x1, Pallas kernels: 113 us -> 98.9 us  [pair_and_fit(): pl.pallas_call(pair_fit_kernel, grid=(blocks,), in_specs=[pl.BlockSpec((S...]
where the time goes in v2:
time: 248 us; the launch traced here: 247 us
  Pallas kernels  240 us (97%)
  local copies, waits for them, and re-layouts  5.41 us (2%)
    pallas_call x1, Pallas kernels, pair_and_fit(): pl.pallas_call(pair_fit_kernel, grid=(blocks,), in_specs=[pl.BlockSpec((S...  98.9 us
    pallas_call x1, Pallas kernels, send_and_project(): pl.pallas_call(project_kernel, out_shape=jax.ShapeDtypeStruct((share, col...  63 us
    pallas_call x1, Pallas kernels, share_rows(): pl.pallas_call(body, out_shape=jax.ShapeDtypeStruct(shape, bf), in_specs=...  43.5 us
    pallas_call x1, Pallas kernels, solve_field(): pl.pallas_call(solve_kernel, out_shape=jax.ShapeDtypeStruct((count, piece...  23 us
    pallas_call x1, Pallas kernels, pick_rows(): pl.pallas_call(pick_kernel, out_shape=jax.ShapeDtypeStruct((npoints, norb...  11.7 us

profile of v2, /device:TPU:0, one launch (start us, length us, event | category | flops | bytes accessed | tf_op | source)
XLA Modules:
  0.0 246.9 jit_solution(5059755463531833769)
XLA Ops:
  0.0 0.7 and_convert_fusion
  0.7 0.1 reshape.34
  0.8 0.1 reduce_max.9.flags_ref
  0.9 0.0 copy-start.3
  0.9 0.7 copy-done.3
  1.6 11.7 %pick_rows.1 = bf16[2048,512]{1,0:T(8,128)(2,1)S(1)} custom-call(s32[2048]{0:T(1024)S(1)} %copy-done.3, s32[256]{0:T(256)S(1)} %reduce_max.9.flags_ref, s32[1]{0:T(128)} %bitcast.offset_ref, bf16[3456,8,512]{2,1,0:T(8,128)(2,1)} %bitcast.14), custom_call_target="tpu_custom_call" | custom-call | tf_op jit(solution)/shard_map/pick_rows/pallas_call | solution.py:356
  13.3 0.0 copy-start.2
  13.3 43.5 %share_rows.1 = bf16[4,2,4,4,16,512]{5,4,3,2,1,0:T(8,128)(2,1)S(1)} custom-call(bf16[4,2,4,4,16,512]{5,4,3,2,1,0:T(8,128)(2,1)S(1)} %bitcast.10), custom_call_target="tpu_custom_call" | custom-call | tf_op jit(solution)/shard_map/share_rows/pallas_call | solution.py:271
  56.8 0.0 copy-done.2
  56.8 98.9 %pair_fit_send.1 = (bf16[18,2048,1536]{2,1,0:T(8,128)(2,1)}, bf16[32,3,96,128]{3,2,1,0:T(8,128)(2,1)}) custom-call(bf16[27648,512]{1,0:T(8,128)(2,1)} %orb_ref.1, bf16[2048,512]{1,0:T(8,128)(2,1)S(1)} %bitcast.11, bf16[32,2048]{1,0:T(8,128)(2,1)S(1)} %bitcast.13), custom_call_target="tpu_custom_call" | custom-call | tf_op jit(solution)/shard_map/pair_fit_send/pallas_call | solution.py:561
  155.7 0.2 sine_convert_fusion
  155.9 0.1 multiply_bitcast_fusion
  156.0 0.1 copy.8.tz_ref
  156.2 0.2 fusion.5
  156.4 0.1 copy.9.ty_ref
  156.5 0.1 copy.10.tyi_ref
  156.6 0.0 copy-start.1
  156.6 1.7 copy-done.1
  158.3 23.0 %solve_field.1.pot_ref = bf16[32,9,24,128]{3,2,1,0:T(8,128)(2,1)S(1)} custom-call(bf16[96,96,128]{2,1,0:T(8,128)(2,1)S(1)} %bitcast.12, bf16[128,256]{1,0:T(8,128)(2,1)S(1)} %copy.8.tz_ref, bf16[96,192]{1,0:T(8,128)(2,1)S(1)} %copy.9.ty_ref, bf16[96,192]{1,0:T(8,128)(2,1)S(1)} %copy.10.tyi_ref, bf16[128,128]{1,0:T(8,128)(2,1)S(1)} %pad_maximum_fusion.3.tzi_ref), custom_call_target="tpu_custom_call" | custom-call | tf_op jit(solution)/shard_map/solve_field/pallas_call | solution.py:701
  181.3 0.0 copy-start
  181.3 1.2 copy-done
  182.5 63.0 %send_project.1 = f32[64,32]{1,0:T(8,128)} custom-call(bf16[32,9,24,128]{3,2,1,0:T(8,128)(2,1)} %copy-done, bf16[18,2048,1536]{2,1,0:T(8,128)(2,1)} %get-tuple-element.8.pair_ref), custom_call_target="tpu_custom_call" | custom-call | tf_op jit(solution)/shard_map/send_project/pallas_call | solution.py:853
  245.5 1.4 copy.11
  (6 shorter events, 0.0 us)
Async XLA Ops:
  0.9 0.7 copy-start.3
  13.3 43.5 %copy-start.2 = (bf16[2048,32]{0,1:T(8,128)(2,1)S(1)}, bf16[2048,32]{0,1:T(8,128)(2,1)}, u32[]{:S(2)}) copy-start(bf16[2048,32]{0,1:T(8,128)(2,1)} %param.4) | copy-start | bytes 393220
  156.6 1.7 copy-start.1
  181.3 1.2 copy-start

commit v3 on v2

--- a/solution.py
+++ b/solution.py
@@ -589,14 +589,40 @@
     )(orbitals, point_rows, panel)
 
 
-GROUP = 8
+GROUP = 24
 HALF = 64
 PIECE = NG * NG // LANES // 3
-
-
-def solve_kernel(field_ref, tz_ref, ty_ref, tyi_ref, tzi_ref, out_ref, by_y, by_x, flat, dense):
+RING = 4
+
+
+def solve_project_kernel(
+    field_ref, tz_ref, ty_ref, tyi_ref, tzi_ref, pair_ref, o_ref,
+    field, by_y, by_x, flat, dense, pot, ring, land, wide, total, parts, held,
+    field_sem, send_sem, recv_sem, own_sem, pair_sem, part_send, part_recv,
+):
     bf = jnp.bfloat16
     f32 = jnp.float32
+    count, me, place = peers_of()
+    blocks, npoints, _ = pair_ref.shape
+    pieces = pot.shape[0]
+    cols = count
+    share = npoints // count
+    planes = NG // count
+    per_piece = blocks // pieces
+    strips = SPAN // LANES
+
+    def load(step):
+        part = pl.ds(step * GROUP, GROUP)
+        return pltpu.make_async_copy(field_ref.at[part], field.at[part], field_sem.at[step])
+
+    def fetch(block):
+        slot = lax.rem(block, RING)
+        return pltpu.make_async_copy(pair_ref.at[block], ring.at[slot], pair_sem.at[slot])
+
+    for step in range(NG // GROUP):
+        load(step).start()
+    greet_all(count, me, place)
+
     lane = lax.broadcasted_iota(jnp.int32, (NG, LANES), 1)
     row = lax.broadcasted_iota(jnp.int32, (NG, LANES), 0)
     sign = jnp.where(lane < HALF, 1.0, -1.0).astype(f32)
@@ -605,17 +631,18 @@
     plane_sq = wave_x * wave_x + wave_z * wave_z
     factor = NG / (2.0 * math.pi) * (NG / (2.0 * math.pi))
 
-    def both(parts):
-        top = jnp.concatenate([part.astype(bf) for part in parts], axis=1)
-        turned = [(pltpu.roll(part, HALF, 1) * sign).astype(bf) for part in parts]
+    def both(shapes):
+        top = jnp.concatenate([part.astype(bf) for part in shapes], axis=1)
+        turned = [(pltpu.roll(part, HALF, 1) * sign).astype(bf) for part in shapes]
         return jnp.concatenate([top, jnp.concatenate(turned, axis=1)], axis=0)
 
-    def cut(wide, k):
-        return wide[:, k * LANES : (k + 1) * LANES]
+    def cut(sheet, k):
+        return sheet[:, k * LANES : (k + 1) * LANES]
 
     def forward(step, carry):
         first = step * GROUP
-        data = field_ref[pl.ds(first, GROUP)].reshape(GROUP * NG, LANES)
+        load(step).wait()
+        data = field[pl.ds(first, GROUP)].reshape(GROUP * NG, LANES)
         a = lax.dot_general(data, tz_ref[...], NN, preferred_element_type=f32).astype(bf)
         top = [a[k * NG : (k + 1) * NG, :LANES] for k in range(GROUP)]
         low = [a[k * NG : (k + 1) * NG, LANES:] for k in range(GROUP)]
@@ -629,10 +656,16 @@
 
     lax.fori_loop(0, NG // GROUP, forward, 0)
 
+    def prime(block, carry):
+        fetch(block).start()
+        return carry
+
+    lax.fori_loop(0, RING, prime, 0)
+
     def middle(step, carry):
         first = step * GROUP
-        parts = [by_y[pl.ds((first + k) * NG, NG), :] for k in range(GROUP)]
-        h = lax.dot_general(ty_ref[...], both(parts), NN, preferred_element_type=f32)
+        rows = [by_y[pl.ds((first + k) * NG, NG), :] for k in range(GROUP)]
+        h = lax.dot_general(ty_ref[...], both(rows), NN, preferred_element_type=f32)
         scaled = []
         for k in range(GROUP):
             index = first + k
@@ -646,126 +679,50 @@
         return carry
 
     lax.fori_loop(0, NG // GROUP, middle, 0)
-
-    planes = NG // out_ref.shape[0]
+    wait_greeted(count)
+
+    def own(piece):
+        return pltpu.make_async_copy(pot.at[piece, me], land.at[piece, me], own_sem.at[piece])
+
+    def send_piece(piece):
+        def body(step, carry):
+            peer = lax.rem(me + step, count)
+            pltpu.make_async_remote_copy(
+                src_ref=pot.at[piece, peer],
+                dst_ref=land.at[piece, me],
+                send_sem=send_sem.at[piece],
+                recv_sem=recv_sem.at[piece],
+                device_id=place(peer),
+                device_id_type=pl.DeviceIdType.MESH,
+            ).start()
+            return carry
+
+        own(piece).start()
+        lax.fori_loop(1, count, body, 0)
+
     quarter = NG // 4
-
-    def backward(step, carry):
-        first = step * GROUP
-        parts = [by_x[pl.ds((first + k) * NG, NG), :] for k in range(GROUP)]
-        p = lax.dot_general(tyi_ref[...], both(parts), NN, preferred_element_type=f32).astype(bf)
-        rows = jnp.concatenate([cut(p, k) for k in range(GROUP)], axis=0)
-        final = lax.dot_general(rows, tzi_ref[...], NN, preferred_element_type=f32)
+    spot = lane[:quarter]
+
+    def backward(local, carry):
+        rows = [by_x[pl.ds((local + planes * k) * NG, NG), :] for k in range(count)]
+        p = lax.dot_general(tyi_ref[...], both(rows), NN, preferred_element_type=f32).astype(bf)
+        tall = jnp.concatenate([cut(p, k) for k in range(count)], axis=0)
+        final = lax.dot_general(tall, tzi_ref[...], NN, preferred_element_type=f32)
         flat[...] = final * f32(1.0 / float(NG**3))
-        for k in range(GROUP):
-            y0, y1, y2, y3 = [
-                flat[pl.ds(k * NG + j, quarter, stride=4), :] for j in range(4)
-            ]
-            spot = lane[:quarter]
-            dense[pl.ds(0, quarter, stride=3), :] = jnp.where(
-                spot < 96, y0, pltpu.roll(y1, 96, 1)
-            )
-            dense[pl.ds(1, quarter, stride=3), :] = jnp.where(
-                spot < 64, pltpu.roll(y1, 96, 1), pltpu.roll(y2, 64, 1)
-            )
-            dense[pl.ds(2, quarter, stride=3), :] = jnp.where(
-                spot < 32, pltpu.roll(y2, 64, 1), pltpu.roll(y3, 32, 1)
-            )
-            index = first + k
+        for k in range(count):
+            y0, y1, y2, y3 = [flat[pl.ds(k * NG + j, quarter, stride=4), :] for j in range(4)]
+            y1, y2, y3 = pltpu.roll(y1, 96, 1), pltpu.roll(y2, 64, 1), pltpu.roll(y3, 32, 1)
+            base = k % 4 * 3 * PIECE
+            dense[pl.ds(base, quarter, stride=3), :] = jnp.where(spot < 96, y0, y1)
+            dense[pl.ds(base + 1, quarter, stride=3), :] = jnp.where(spot < 64, y1, y2)
+            dense[pl.ds(base + 2, quarter, stride=3), :] = jnp.where(spot < 32, y2, y3)
             for m in range(3):
-                out_ref[index // planes, lax.rem(index, planes) * 3 + m] = dense[
-                    m * PIECE : (m + 1) * PIECE, :
-                ].astype(bf)
-        return carry
-
-    lax.fori_loop(0, NG // GROUP, backward, 0)
-
-
-def solve_field(field, count):
-    bf = jnp.bfloat16
-    f32 = jnp.float32
-    cos_tab, sin_tab = wave_tables(NG)
-    keep = NG // 2 + 1
-
-    def wide(table):
-        return jnp.pad(table[:, :keep], ((0, LANES - NG), (0, HALF - keep)))
-
-    cz, sz = wide(cos_tab), wide(sin_tab)
-    tz = jnp.concatenate([cz, -sz, -sz, -cz], axis=1)
-    ty = jnp.concatenate([cos_tab, sin_tab], axis=1)
-    tyi = jnp.concatenate([cos_tab, -sin_tab], axis=1)
-    spot = lax.iota(jnp.int32, HALF)[:, None]
-    weight = jnp.where((spot == 0) | (spot == NG // 2), 1.0, 2.0).astype(bf)
-    tzi = jnp.concatenate([cz.T * weight, -(sz.T * weight)], axis=0)
-    pieces = NG // count * 3
-    return pl.pallas_call(
-        solve_kernel,
-        out_shape=jax.ShapeDtypeStruct((count, pieces, PIECE, LANES), bf),
-        in_specs=[pl.BlockSpec(memory_space=pltpu.VMEM)] * 5,
-        out_specs=pl.BlockSpec(memory_space=pltpu.VMEM),
-        scratch_shapes=[
-            pltpu.VMEM((NG * NG, LANES), f32),
-            pltpu.VMEM((NG * NG, LANES), f32),
-            pltpu.VMEM((GROUP * NG, LANES), f32),
-            pltpu.VMEM((3 * PIECE, LANES), f32),
-        ],
-        compiler_params=pltpu.CompilerParams(vmem_limit_bytes=40 << 20),
-        name="solve_field",
-    )(field.reshape(NG, NG, LANES), tz, ty, tyi, tzi)
-
-
-RING = 6
-
-
-def project_kernel(
-    pot_ref, pair_ref, o_ref, ring, land, wide, total, parts, held,
-    send_sem, recv_sem, own_sem, pair_sem, part_send, part_recv,
-):
-    bf = jnp.bfloat16
-    f32 = jnp.float32
-    count, me, place = peers_of()
-    blocks, npoints, _ = pair_ref.shape
-    pieces = pot_ref.shape[1]
-    cols = count
-    share = npoints // count
-    per_piece = blocks // pieces
-    strips = SPAN // LANES
-
-    def fetch(block):
-        slot = lax.rem(block, RING)
-        return pltpu.make_async_copy(pair_ref.at[block], ring.at[slot], pair_sem.at[slot])
-
-    def prime(block, carry):
-        fetch(block).start()
-        return carry
-
-    greet_all(count, me, place)
-    lax.fori_loop(0, RING, prime, 0)
-    wait_greeted(count)
-
-    def copy(piece, step):
-        peer = lax.rem(me + step, count)
-        return pltpu.make_async_remote_copy(
-            src_ref=pot_ref.at[peer, piece],
-            dst_ref=land.at[piece, me],
-            send_sem=send_sem.at[piece],
-            recv_sem=recv_sem.at[piece],
-            device_id=place(peer),
-            device_id_type=pl.DeviceIdType.MESH,
-        )
-
-    def own(piece):
-        return pltpu.make_async_copy(pot_ref.at[me, piece], land.at[piece, me], own_sem.at[piece])
-
-    def send_piece(piece, carry):
-        def body(step, inner):
-            copy(piece, step).start()
-            return inner
-
-        own(piece).start()
-        return lax.fori_loop(1, count, body, carry)
-
-    lax.fori_loop(0, pieces, send_piece, 0)
+                pot[local * 3 + m, k] = dense[base + m * PIECE : base + (m + 1) * PIECE, :].astype(bf)
+        for m in range(3):
+            send_piece(local * 3 + m)
+        return carry
+
+    lax.fori_loop(0, planes, backward, 0)
     total[...] = jnp.zeros_like(total)
 
     def work(piece, carry):
@@ -820,7 +777,7 @@
     held[me] = parts[me]
 
     def drain_piece(piece, carry):
-        sent = pot_ref.at[pl.ds(0, count - 1), piece]
+        sent = pot.at[piece, pl.ds(0, count - 1)]
         pltpu.make_async_copy(sent, sent, send_sem.at[piece]).wait()
         return carry
 
@@ -833,8 +790,8 @@
 
     lax.fori_loop(1, count, part_receive, 0)
     summed = jnp.sum(held[...], axis=0)
-    both = jnp.concatenate([summed, pltpu.roll(summed, share, 1)], axis=0)
-    o_ref[...] = both.T[:share, :]
+    pile = jnp.concatenate([summed, pltpu.roll(summed, share, 1)], axis=0)
+    o_ref[...] = pile.T[:share, :]
 
     def part_drain(step, carry):
         part_copy(step, lax.rem(me + step, count), me).wait_send()
@@ -843,25 +800,46 @@
     lax.fori_loop(1, count, part_drain, 0)
 
 
-def send_and_project(potential, pair):
+def solve_and_project(field, pair, count):
     bf = jnp.bfloat16
     f32 = jnp.float32
-    count, pieces = potential.shape[:2]
+    cos_tab, sin_tab = wave_tables(NG)
+    keep = NG // 2 + 1
+
+    def padded(table):
+        return jnp.pad(table[:, :keep], ((0, LANES - NG), (0, HALF - keep)))
+
+    cz, sz = padded(cos_tab), padded(sin_tab)
+    tz = jnp.concatenate([cz, -sz, -sz, -cz], axis=1)
+    ty = jnp.concatenate([cos_tab, sin_tab], axis=1)
+    tyi = jnp.concatenate([cos_tab, -sin_tab], axis=1)
+    spot = lax.iota(jnp.int32, HALF)[:, None]
+    weight = jnp.where((spot == 0) | (spot == NG // 2), 1.0, 2.0).astype(bf)
+    tzi = jnp.concatenate([cz.T * weight, -(sz.T * weight)], axis=0)
+    pieces = NG // count * 3
     blocks, npoints, span = pair.shape
     cols = count
-    share = npoints // count
+    any_spec = pl.BlockSpec(memory_space=pl.ANY)
+    vmem_spec = pl.BlockSpec(memory_space=pltpu.VMEM)
     return pl.pallas_call(
-        project_kernel,
-        out_shape=jax.ShapeDtypeStruct((share, cols), f32),
-        in_specs=[pl.BlockSpec(memory_space=pltpu.VMEM), pl.BlockSpec(memory_space=pl.ANY)],
-        out_specs=pl.BlockSpec(memory_space=pltpu.VMEM),
+        solve_project_kernel,
+        out_shape=jax.ShapeDtypeStruct((npoints // count, cols), f32),
+        in_specs=[any_spec] + [vmem_spec] * 4 + [any_spec],
+        out_specs=vmem_spec,
         scratch_shapes=[
+            pltpu.VMEM((NG, NG, LANES), bf),
+            pltpu.VMEM((NG * NG, LANES), f32),
+            pltpu.VMEM((NG * NG, LANES), f32),
+            pltpu.VMEM((count * NG, LANES), f32),
+            pltpu.VMEM((4 * 3 * PIECE, LANES), f32),
+            pltpu.VMEM((pieces, count, PIECE, LANES), bf),
             pltpu.VMEM((RING, npoints, span), bf),
             pltpu.VMEM((pieces, count, PIECE, LANES), bf),
             pltpu.VMEM((cols * PIECE, LANES), f32),
             pltpu.VMEM((cols, npoints), f32),
             pltpu.VMEM((count, cols // 2, LANES), f32),
             pltpu.VMEM((count, cols // 2, LANES), f32),
+            pltpu.SemaphoreType.DMA((NG // GROUP,)),
             pltpu.SemaphoreType.DMA((pieces,)),
             pltpu.SemaphoreType.DMA((pieces,)),
             pltpu.SemaphoreType.DMA((pieces,)),
@@ -870,10 +848,10 @@
             pltpu.SemaphoreType.DMA((count,)),
         ],
         compiler_params=pltpu.CompilerParams(
-            collective_id=2, has_side_effects=True, vmem_limit_bytes=54 << 20
+            collective_id=2, has_side_effects=True, vmem_limit_bytes=60 << 20
         ),
-        name="send_project",
-    )(potential, pair)
+        name="solve_project",
+    )(field.reshape(NG, NG, LANES), tz, ty, tyi, tzi, pair)
 
 
 def fits_planes(rows, npoints, cols, count):
@@ -901,7 +879,7 @@
 
     if fits_planes(row_count, npoints, inverse_panel.shape[1], grid_count * vec_count):
         pair, field = pair_and_fit(orbitals, point_rows, inverse_panel.T)
-        return send_and_project(solve_field(field, grid_count * vec_count), pair)
+        return solve_and_project(field, pair, grid_count * vec_count)
 
     def pair_block(block):
         correlation = lax.dot_general(

time: 248 us -> 234 us (0.944)
  Pallas kernels: 240 us -> 227 us
    pallas_call x2 -> x1, Pallas kernels: 86 us -> 73.3 us  [solve_and_project(): pl.pallas_call(solve_project_kernel, out_shape=jax.ShapeDtypeStruct((npoi...]
    unnamed x8 -> x4, local copies, waits for them, and re-layouts: 3.57 us -> 0.7 us
where the time goes in v3:
time: 234 us
  Pallas kernels  227 us (97%)
  local copies, waits for them, and re-layouts  4.4 us (2%)
    pallas_call x1, Pallas kernels, pair_and_fit(): pl.pallas_call(pair_fit_kernel, grid=(blocks,), in_specs=[pl.BlockSpec((S...  98.2 us
    pallas_call x1, Pallas kernels, solve_and_project(): pl.pallas_call(solve_project_kernel, out_shape=jax.ShapeDtypeStruct((npoi...  73.3 us
    pallas_call x1, Pallas kernels, share_rows(): pl.pallas_call(body, out_shape=jax.ShapeDtypeStruct(shape, bf), in_specs=...  43.3 us
    pallas_call x1, Pallas kernels, pick_rows(): pl.pallas_call(pick_kernel, out_shape=jax.ShapeDtypeStruct((npoints, norb...  12.2 us

profile of v3, /device:TPU:0, one launch (start us, length us, event | category | flops | bytes accessed | tf_op | source)
XLA Modules:
  0.0 233.5 jit_solution(2748540561458933397)
XLA Ops:
  0.0 0.7 and_convert_fusion
  0.7 0.1 reshape.34
  0.8 0.1 reduce_max.9.flags_ref
  0.9 0.0 copy-start.1
  0.9 0.7 copy-done.1
  1.6 12.2 %pick_rows.1 = bf16[2048,512]{1,0:T(8,128)(2,1)S(1)} custom-call(s32[2048]{0:T(1024)S(1)} %copy-done.1, s32[256]{0:T(256)S(1)} %reduce_max.9.flags_ref, s32[1]{0:T(128)} %bitcast.offset_ref, bf16[3456,8,512]{2,1,0:T(8,128)(2,1)} %bitcast.13), custom_call_target="tpu_custom_call" | custom-call | tf_op jit(solution)/shard_map/pick_rows/pallas_call | solution.py:356
  13.9 0.0 copy-start
  13.9 43.3 %share_rows.1 = bf16[4,2,4,4,16,512]{5,4,3,2,1,0:T(8,128)(2,1)S(1)} custom-call(bf16[4,2,4,4,16,512]{5,4,3,2,1,0:T(8,128)(2,1)S(1)} %bitcast.10), custom_call_target="tpu_custom_call" | custom-call | tf_op jit(solution)/shard_map/share_rows/pallas_call | solution.py:271
  57.1 0.0 copy-done
  57.1 98.2 %pair_fit_send.1 = (bf16[18,2048,1536]{2,1,0:T(8,128)(2,1)}, bf16[32,3,96,128]{3,2,1,0:T(8,128)(2,1)}) custom-call(bf16[27648,512]{1,0:T(8,128)(2,1)} %orb_ref.1, bf16[2048,512]{1,0:T(8,128)(2,1)S(1)} %bitcast.11, bf16[32,2048]{1,0:T(8,128)(2,1)S(1)} %bitcast.12), custom_call_target="tpu_custom_call" | custom-call | tf_op jit(solution)/shard_map/pair_fit_send/pallas_call | solution.py:561
  155.4 0.2 sine_convert_fusion
  155.6 0.1 multiply_bitcast_fusion
  155.7 0.7 copy.8.tz_ref
  156.5 0.2 fusion.5
  156.7 0.7 copy.9.ty_ref
  157.4 0.7 copy.10.tyi_ref
  158.1 0.6 pad_maximum_fusion.3.tzi_ref
  158.7 73.3 %solve_project.1 = f32[64,32]{1,0:T(8,128)} custom-call(bf16[96,96,128]{2,1,0:T(8,128)(2,1)} %bitcast.14, bf16[128,256]{1,0:T(8,128)(2,1)} %copy.8.tz_ref, bf16[96,192]{1,0:T(8,128)(2,1)} %copy.9.ty_ref, bf16[96,192]{1,0:T(8,128)(2,1)} %copy.10.tyi_ref, bf16[128,128]{1,0:T(8,128)(2,1)} %pad_maximum_fusion.3.tzi_ref, ...), custom_call_target="tpu_custom_call" | custom-call | tf_op jit(solution)/shard_map/solve_project/pallas_call | solution.py:824
  232.1 1.4 copy.11
  (5 shorter events, 0.0 us)
Async XLA Ops:
  0.9 0.7 copy-start.1
  13.9 43.3 %copy-start = (bf16[2048,32]{0,1:T(8,128)(2,1)S(1)}, bf16[2048,32]{0,1:T(8,128)(2,1)}, u32[]{:S(2)}) copy-start(bf16[2048,32]{0,1:T(8,128)(2,1)} %param.4) | copy-start | bytes 393220

commit v4 on v3

--- a/solution.py
+++ b/solution.py
@@ -2,6 +2,7 @@
 
 import jax
 import jax.numpy as jnp
+import numpy as np
 from jax import lax
 from jax.experimental import pallas as pl
 from jax.experimental.pallas import tpu as pltpu
@@ -18,6 +19,13 @@
     phase = index[:, None] * index[None, :] % count
     angle = phase.astype(jnp.float32) * (2.0 * math.pi / count)
     return (jnp.cos(angle).astype(jnp.bfloat16), jnp.sin(angle).astype(jnp.bfloat16))
+
+
+def literal_tables(count):
+    index = np.arange(count)
+    phase = index[:, None] * index[None, :] % count
+    angle = phase.astype(np.float32) * np.float32(2.0 * math.pi / count)
+    return np.cos(angle).astype(jnp.bfloat16), np.sin(angle).astype(jnp.bfloat16)
 
 
 def wavenumber(index, count):
@@ -140,7 +148,13 @@
     )(blocks)
 
 
-def share_kernel(chunks, x_ref, o_ref, near, wide, far, sum1, sum2, sum3, sends, recvs, own_sem):
+def share_kernel(chunks, early, refs):
+    if early:
+        x_ref, panel_ref, orb_ref, o_ref, early_ref, fit_ref = refs[:6]
+        orbs, pairs, orb_sem, pair_sem = refs[-4:]
+        near, wide, far, sum1, sum2, sum3, sends, recvs, own_sem = refs[6:-4]
+    else:
+        x_ref, o_ref, near, wide, far, sum1, sum2, sum3, sends, recvs, own_sem = refs
     bf = jnp.bfloat16
     f32 = jnp.float32
     vec_count = lax.axis_size("vec")
@@ -236,6 +250,29 @@
         if stage == 4:
             own(c).wait()
 
+    def fetch():
+        return pltpu.make_async_copy(orb_ref.at[pl.ds(0, early)], orbs, orb_sem)
+
+    def keep(c):
+        height = pairs.shape[1] // chunks
+        part = pl.ds(c * height, height)
+        return pltpu.make_async_copy(
+            pairs.at[:, part], early_ref.at[:, part], pair_sem.at[c]
+        )
+
+    def multiply(c):
+        height = pairs.shape[1] // chunks
+        rows = o_ref[c].reshape(height, o_ref.shape[-1])
+
+        def body(e, carry):
+            part = lax.dot_general(rows, orbs[e], NT, preferred_element_type=f32)
+            pairs[e, c * height : (c + 1) * height, :] = (part * part).astype(bf)
+            return carry
+
+        lax.fori_loop(0, early, body, 0)
+
+    if early:
+        fetch().start()
     for tick in range(chunks + 6):
         for stage in range(6, -1, -1):
             c = tick - stage
@@ -245,6 +282,22 @@
                 if stage < 6:
                     for move in copies(stage, c):
                         move.start()
+        if early and tick >= 6:
+            if tick == 6:
+                fetch().wait()
+            multiply(tick - 6)
+            keep(tick - 6).start()
+    if early:
+
+        def fit(e, carry):
+            fit_ref[e] = lax.dot_general(
+                panel_ref[...], pairs[e], NN, preferred_element_type=f32
+            )
+            return carry
+
+        lax.fori_loop(0, early, fit, 0)
+        for c in range(chunks):
+            keep(c).wait()
     for c in range(chunks):
         for stage in range(6):
             for move in copies(stage, c):
@@ -254,41 +307,65 @@
 ROWS = 16
 
 
-def share_rows(picked, grid_count, vec_count):
+def share_rows(picked, grid_count, vec_count, panel=None, orbitals=None):
     bf = jnp.bfloat16
     npoints, norb = picked.shape
     count = grid_count * vec_count
     if npoints % (count * ROWS) != 0 or grid_count % 2 != 0:
         return lax.psum(picked.astype(jnp.float32), ("grid", "vec")).astype(picked.dtype)
+    early = 0 if panel is None else EARLY
     chunks = npoints // (count * ROWS)
     deep = grid_count // 2
     shape = (chunks, 2, vec_count, deep, ROWS, norb)
     slots = chunks * (2 + 2 * (vec_count - 1) + 2 * (deep - 1))
+    vmem_spec = pl.BlockSpec(memory_space=pltpu.VMEM)
+    any_spec = pl.BlockSpec(memory_space=pl.ANY)
+    args = [picked.reshape(shape)]
+    in_specs, out_specs = [vmem_spec], [vmem_spec]
+    out_shape = [jax.ShapeDtypeStruct(shape, bf)]
+    scratch = [
+        pltpu.VMEM((chunks, vec_count, deep, ROWS, norb), bf),
+        pltpu.VMEM((chunks, vec_count - 1, deep, ROWS, norb), bf),
+        pltpu.VMEM((chunks, deep - 1, ROWS, norb), bf),
+        pltpu.VMEM((chunks, vec_count, deep, ROWS, norb), bf),
+        pltpu.VMEM((chunks, deep, ROWS, norb), bf),
+        pltpu.VMEM((chunks, ROWS, norb), bf),
+        pltpu.SemaphoreType.DMA((slots,)),
+        pltpu.SemaphoreType.DMA((slots,)),
+        pltpu.SemaphoreType.DMA((chunks,)),
+    ]
+    if early:
+        cols = panel.shape[0]
+        args += [panel, orbitals.reshape(-1, SPAN, norb)]
+        in_specs += [vmem_spec, any_spec]
+        out_specs += [any_spec, vmem_spec]
+        out_shape += [
+            jax.ShapeDtypeStruct((early, npoints, SPAN), bf),
+            jax.ShapeDtypeStruct((early, cols, SPAN), jnp.float32),
+        ]
+        scratch += [
+            pltpu.VMEM((early, SPAN, norb), bf),
+            pltpu.VMEM((early, npoints, SPAN), bf),
+            pltpu.SemaphoreType.DMA(()),
+            pltpu.SemaphoreType.DMA((chunks,)),
+        ]
 
     def body(*refs):
-        share_kernel(chunks, *refs)
-
-    return pl.pallas_call(
+        share_kernel(chunks, early, refs)
+
+    outs = pl.pallas_call(
         body,
-        out_shape=jax.ShapeDtypeStruct(shape, bf),
-        in_specs=[pl.BlockSpec(memory_space=pltpu.VMEM)],
-        out_specs=pl.BlockSpec(memory_space=pltpu.VMEM),
-        scratch_shapes=[
-            pltpu.VMEM((chunks, vec_count, deep, ROWS, norb), bf),
-            pltpu.VMEM((chunks, vec_count - 1, deep, ROWS, norb), bf),
-            pltpu.VMEM((chunks, deep - 1, ROWS, norb), bf),
-            pltpu.VMEM((chunks, vec_count, deep, ROWS, norb), bf),
-            pltpu.VMEM((chunks, deep, ROWS, norb), bf),
-            pltpu.VMEM((chunks, ROWS, norb), bf),
-            pltpu.SemaphoreType.DMA((slots,)),
-            pltpu.SemaphoreType.DMA((slots,)),
-            pltpu.SemaphoreType.DMA((chunks,)),
-        ],
+        out_shape=out_shape,
+        in_specs=in_specs,
+        out_specs=out_specs,
+        scratch_shapes=scratch,
         compiler_params=pltpu.CompilerParams(
-            collective_id=4, has_side_effects=True, vmem_limit_bytes=32 << 20
+            collective_id=4, has_side_effects=True, vmem_limit_bytes=46 << 20
         ),
         name="share_rows",
-    )(picked.reshape(shape)).reshape(npoints, norb)
+    )(*args)
+    rows = outs[0].reshape(npoints, norb)
+    return (rows, outs[1], outs[2]) if early else rows
 
 
 OCTET = 8
@@ -319,7 +396,9 @@
     def scan(group, held):
         return lax.cond(
             flags_ref[group] > 0,
-            lambda h: lax.fori_loop(0, OCTET, lambda k, n: look(group * OCTET + k, n), h),
+            lambda h: lax.fori_loop(
+                0, OCTET, lambda k, n: look(group * OCTET + k, n), h, unroll=True
+            ),
             lambda h: h,
             held,
         )
@@ -370,7 +449,7 @@
             pltpu.VMEM((npoints, norb), jnp.float32),
             pltpu.SemaphoreType.DMA(()),
         ],
-        compiler_params=pltpu.CompilerParams(vmem_limit_bytes=40 << 20),
+        compiler_params=pltpu.CompilerParams(vmem_limit_bytes=28 << 20),
         name="pick_rows",
     )(points, flags, offset[None].astype(jnp.int32), orbitals.reshape(rows // OCTET, OCTET, norb))
 
@@ -427,15 +506,16 @@
 SPAN = LINES * NG
 TAKE = 512
 JOIN = 3
+EARLY = 4
 
 
 def pair_fit_kernel(
-    orb_ref, rows_ref, panel_ref, pair_ref, field_ref, fit_buf, fit_rows, out_buf,
+    orb_ref, rows_ref, panel_ref, early_ref, pair_ref, field_ref, fit_buf, fit_rows, out_buf,
     send_sem, recv_sem, own_sem,
 ):
     bf = jnp.bfloat16
-    block = pl.program_id(0)
-    blocks = pl.num_programs(0)
+    block = pl.program_id(0) + EARLY
+    blocks = pl.num_programs(0) + EARLY
     count, me, place = peers_of()
     npoints = rows_ref.shape[0]
     cols = panel_ref.shape[0]
@@ -472,15 +552,11 @@
         pltpu.make_async_copy(mine, mine, own_sem.at[slot]).wait()
         pltpu.make_async_copy(sent, sent, send_sem.at[slot]).wait()
 
-    @pl.when(block == 0)
+    @pl.when(block == EARLY)
     def _():
         greet_all(count, me, place)
 
-    @pl.when(block == 1)
-    def _():
-        wait_greeted(count)
-
-    before = jnp.maximum(block - 1, 0)
+    before = block - 1
 
     @pl.when((block > 2 * JOIN) & (lax.rem(before, JOIN) == 0))
     def _():
@@ -503,22 +579,32 @@
             if turn:
                 wide = pltpu.roll(wide, 2 * LANES - turn, 1)
             fit_rows[pl.ds(line, cols, stride=LINES), :] = wide[:, :LANES]
-        slot = lax.rem(index // JOIN, 2)
-        begin = pl.multiple_of(lax.rem(index, JOIN) * LINES, LINES)
+        slot = index // JOIN % 2
+        begin = index % JOIN * LINES
+        if not isinstance(index, int):
+            begin = pl.multiple_of(begin, LINES)
         out_buf[slot, :, pl.ds(begin, LINES), :] = (
             fit_rows[...].astype(bf).reshape(cols, LINES, LANES)
         )
 
-    @pl.when(block == 0)
+    @pl.when(block == EARLY)
     def _():
-        fit_buf[...] = jnp.zeros_like(fit_buf)
+        for index in range(EARLY - 1):
+            fit_buf[...] = early_ref[index]
+            arrange(index)
+        fit_buf[...] = early_ref[EARLY - 1]
 
     multiply(0)
     arrange(before)
     for first in range(TAKE, npoints // 2, TAKE):
         multiply(first)
 
-    @pl.when((block >= JOIN) & (lax.rem(block, JOIN) == 0))
+    @pl.when(block == EARLY)
+    def _():
+        wait_greeted(count)
+        send(0, 0, tall)
+
+    @pl.when((block > EARLY) & (lax.rem(block, JOIN) == 0))
     def _():
         send(block // JOIN - 1, 0, tall)
 
@@ -550,21 +636,22 @@
         drain(groups - 1)
 
 
-def pair_and_fit(orbitals, point_rows, panel):
+def pair_and_fit(orbitals, point_rows, panel, early_fit):
     bf = jnp.bfloat16
     rows, norb = orbitals.shape
     npoints = point_rows.shape[0]
     cols = panel.shape[0]
-    blocks = rows // SPAN
+    blocks = rows // SPAN - EARLY
     planes = rows // (NG * NG)
     count = lax.axis_size("grid") * lax.axis_size("vec")
     return pl.pallas_call(
         pair_fit_kernel,
         grid=(blocks,),
         in_specs=[
-            pl.BlockSpec((SPAN, norb), lambda i: (i, 0)),
+            pl.BlockSpec((SPAN, norb), lambda i: (i + EARLY, 0)),
             pl.BlockSpec((npoints, norb), lambda i: (0, 0)),
             pl.BlockSpec((cols, npoints), lambda i: (0, 0)),
+            pl.BlockSpec((EARLY, cols, SPAN), lambda i: (0, 0, 0)),
         ],
         out_specs=[
             pl.BlockSpec((1, npoints, SPAN), lambda i: (i, 0, 0)),
@@ -583,27 +670,28 @@
             pltpu.SemaphoreType.DMA((2,)),
         ],
         compiler_params=pltpu.CompilerParams(
-            collective_id=1, has_side_effects=True, vmem_limit_bytes=50 << 20
+            collective_id=1, has_side_effects=True, vmem_limit_bytes=36 << 20
         ),
         name="pair_fit_send",
-    )(orbitals, point_rows, panel)
+    )(orbitals, point_rows, panel, early_fit)
 
 
 GROUP = 24
 HALF = 64
 PIECE = NG * NG // LANES // 3
-RING = 4
+RING = EARLY
 
 
 def solve_project_kernel(
-    field_ref, tz_ref, ty_ref, tyi_ref, tzi_ref, pair_ref, o_ref,
+    field_ref, tz_ref, ty_ref, tyi_ref, tzi_ref, early_ref, pair_ref, o_ref,
     field, by_y, by_x, flat, dense, pot, ring, land, wide, total, parts, held,
     field_sem, send_sem, recv_sem, own_sem, pair_sem, part_send, part_recv,
 ):
     bf = jnp.bfloat16
     f32 = jnp.float32
     count, me, place = peers_of()
-    blocks, npoints, _ = pair_ref.shape
+    rest, npoints, _ = pair_ref.shape
+    blocks = rest + EARLY
     pieces = pot.shape[0]
     cols = count
     share = npoints // count
@@ -615,9 +703,9 @@
         part = pl.ds(step * GROUP, GROUP)
         return pltpu.make_async_copy(field_ref.at[part], field.at[part], field_sem.at[step])
 
-    def fetch(block):
+    def fetch(ref, block):
         slot = lax.rem(block, RING)
-        return pltpu.make_async_copy(pair_ref.at[block], ring.at[slot], pair_sem.at[slot])
+        return pltpu.make_async_copy(ref.at[block], ring.at[slot], pair_sem.at[slot])
 
     for step in range(NG // GROUP):
         load(step).start()
@@ -657,10 +745,10 @@
     lax.fori_loop(0, NG // GROUP, forward, 0)
 
     def prime(block, carry):
-        fetch(block).start()
-        return carry
-
-    lax.fori_loop(0, RING, prime, 0)
+        fetch(early_ref, block).start()
+        return carry
+
+    lax.fori_loop(0, EARLY, prime, 0)
 
     def middle(step, carry):
         first = step * GROUP
@@ -733,7 +821,7 @@
         for half in range(per_piece):
             block = piece * per_piece + half
             slot = lax.rem(block, RING)
-            fetch(block).wait()
+            pltpu.make_async_copy(ring.at[slot], ring.at[slot], pair_sem.at[slot]).wait()
             lines = [
                 wide[pl.ds(half * strips + j, cols, stride=PIECE), :].astype(bf)
                 for j in range(strips)
@@ -742,9 +830,9 @@
                 jnp.concatenate(lines, axis=1), ring[slot], NT, preferred_element_type=f32
             )
 
-            @pl.when(block + RING < blocks)
+            @pl.when(block < rest)
             def _():
-                fetch(block + RING).start()
+                fetch(pair_ref, block).start()
 
         return carry
 
@@ -800,22 +888,23 @@
     lax.fori_loop(1, count, part_drain, 0)
 
 
-def solve_and_project(field, pair, count):
+def solve_and_project(field, early, pair, count):
     bf = jnp.bfloat16
     f32 = jnp.float32
-    cos_tab, sin_tab = wave_tables(NG)
+    cos_tab, sin_tab = literal_tables(NG)
     keep = NG // 2 + 1
 
     def padded(table):
-        return jnp.pad(table[:, :keep], ((0, LANES - NG), (0, HALF - keep)))
+        return np.pad(table[:, :keep], ((0, LANES - NG), (0, HALF - keep)))
 
     cz, sz = padded(cos_tab), padded(sin_tab)
-    tz = jnp.concatenate([cz, -sz, -sz, -cz], axis=1)
-    ty = jnp.concatenate([cos_tab, sin_tab], axis=1)
-    tyi = jnp.concatenate([cos_tab, -sin_tab], axis=1)
-    spot = lax.iota(jnp.int32, HALF)[:, None]
-    weight = jnp.where((spot == 0) | (spot == NG // 2), 1.0, 2.0).astype(bf)
-    tzi = jnp.concatenate([cz.T * weight, -(sz.T * weight)], axis=0)
+    tz = np.concatenate([cz, -sz, -sz, -cz], axis=1)
+    ty = np.concatenate([cos_tab, sin_tab], axis=1)
+    tyi = np.concatenate([cos_tab, -sin_tab], axis=1)
+    spot = np.arange(HALF)[:, None]
+    weight = np.where((spot == 0) | (spot == NG // 2), 1.0, 2.0).astype(bf)
+    tzi = np.concatenate([cz.T * weight, -(sz.T * weight)], axis=0)
+    tz, ty, tyi, tzi = [jnp.asarray(table, bf) for table in (tz, ty, tyi, tzi)]
     pieces = NG // count * 3
     blocks, npoints, span = pair.shape
     cols = count
@@ -824,7 +913,7 @@
     return pl.pallas_call(
         solve_project_kernel,
         out_shape=jax.ShapeDtypeStruct((npoints // count, cols), f32),
-        in_specs=[any_spec] + [vmem_spec] * 4 + [any_spec],
+        in_specs=[any_spec] + [vmem_spec] * 4 + [any_spec] * 2,
         out_specs=vmem_spec,
         scratch_shapes=[
             pltpu.VMEM((NG, NG, LANES), bf),
@@ -848,10 +937,10 @@
             pltpu.SemaphoreType.DMA((count,)),
         ],
         compiler_params=pltpu.CompilerParams(
-            collective_id=2, has_side_effects=True, vmem_limit_bytes=60 << 20
+            collective_id=2, has_side_effects=True, vmem_limit_bytes=54 << 20
         ),
         name="solve_project",
-    )(field.reshape(NG, NG, LANES), tz, ty, tyi, tzi, pair)
+    )(field.reshape(NG, NG, LANES), tz, ty, tyi, tzi, early, pair)
 
 
 def fits_planes(rows, npoints, cols, count):
@@ -860,7 +949,9 @@
         cols == count
         and rows % (NG * NG) == 0
         and NG % (rows // (NG * NG)) == 0
-        and blocks >= max(RING, 2 * JOIN)
+        and blocks >= EARLY + 2 * JOIN
+        and EARLY > JOIN
+        and npoints % (count * ROWS) == 0
         and NG // LINES % JOIN == 0
         and npoints % TAKE == 0
         and 2 * npoints == count * LANES
@@ -875,11 +966,13 @@
     npoints = points.shape[0]
     offset = (lax.axis_index("grid") * vec_count + lax.axis_index("vec")) * row_count
     picked = pick_rows(orbitals, points, offset)
+    cols = inverse_panel.shape[1]
+    if fits_planes(row_count, npoints, cols, grid_count * vec_count):
+        panel = inverse_panel.T
+        point_rows, early, early_fit = share_rows(picked, grid_count, vec_count, panel, orbitals)
+        pair, field = pair_and_fit(orbitals, point_rows, panel, early_fit)
+        return solve_and_project(field, early, pair, grid_count * vec_count)
     point_rows = share_rows(picked, grid_count, vec_count)
-
-    if fits_planes(row_count, npoints, inverse_panel.shape[1], grid_count * vec_count):
-        pair, field = pair_and_fit(orbitals, point_rows, inverse_panel.T)
-        return solve_and_project(field, pair, grid_count * vec_count)
 
     def pair_block(block):
         correlation = lax.dot_general(

time: 234 us -> 224 us (0.957)
  Pallas kernels: 227 us -> 219 us
    pallas_call x1, Pallas kernels: 98.2 us -> 80.4 us  [pair_and_fit(): pl.pallas_call(pair_fit_kernel, grid=(blocks,), in_specs=[pl.BlockSpec((S...]
    pallas_call x1, Pallas kernels: 43.3 us -> 54.6 us  [share_rows(): pl.pallas_call(body, out_shape=out_shape, in_specs=in_specs, out_specs=ou...]
where the time goes in v4:
time: 224 us
  Pallas kernels  219 us (98%)
  local copies, waits for them, and re-layouts  3.69 us (2%)
    pallas_call x1, Pallas kernels, pair_and_fit(): pl.pallas_call(pair_fit_kernel, grid=(blocks,), in_specs=[pl.BlockSpec((S...  80.4 us
    pallas_call x1, Pallas kernels, solve_and_project(): pl.pallas_call(solve_project_kernel, out_shape=jax.ShapeDtypeStruct((npoi...  73.1 us
    pallas_call x1, Pallas kernels, share_rows(): pl.pallas_call(body, out_shape=out_shape, in_specs=in_specs, out_specs=ou...  54.6 us
    pallas_call x1, Pallas kernels, pick_rows(): pl.pallas_call(pick_kernel, out_shape=jax.ShapeDtypeStruct((npoints, norb...  11.1 us

profile of v4, /device:TPU:0, one launch (start us, length us, event | category | flops | bytes accessed | tf_op | source)
XLA Modules:
  0.0 223.8 jit_solution(10012068446060351366)
XLA Ops:
  0.0 0.0 copy-start.1
  0.0 0.7 and_convert_fusion
  0.7 0.1 reshape.23
  0.8 0.1 reduce_max.9.flags_ref
  1.0 0.0 copy-start.2
  1.0 0.7 copy-done.2
  1.7 11.1 %pick_rows.1 = bf16[2048,512]{1,0:T(8,128)(2,1)S(1)} custom-call(s32[2048]{0:T(1024)S(1)} %copy-done.2, s32[256]{0:T(256)S(1)} %reduce_max.9.flags_ref, s32[1]{0:T(128)} %bitcast.offset_ref, bf16[3456,8,512]{2,1,0:T(8,128)(2,1)} %bitcast.12), custom_call_target="tpu_custom_call" | custom-call | tf_op jit(solution)/shard_map/pick_rows/pallas_call | solution.py:435
  12.8 0.0 copy-done.1
  12.8 54.6 %share_rows.1 = (bf16[4,2,4,4,16,512]{5,4,3,2,1,0:T(8,128)(2,1)S(1)}, bf16[4,2048,1536]{2,1,0:T(8,128)(2,1)}, f32[4,32,1536]{2,1,0:T(8,128)S(1)}) custom-call(bf16[4,2,4,4,16,512]{5,4,3,2,1,0:T(8,128)(2,1)S(1)} %bitcast.7, bf16[32,2048]{1,0:T(8,128)(2,1)S(1)} %bitcast.10, bf16[18,1536,512]{2,1,0:T(8,128)(2,1)} %bitcast.13), custom_call_target="tpu_custom_call" | custom-call | tf_op jit(solution)/shard_map/share_rows/pallas_call | solution.py:356
  67.4 80.4 %pair_fit_send.1 = (bf16[14,2048,1536]{2,1,0:T(8,128)(2,1)}, bf16[32,3,96,128]{3,2,1,0:T(8,128)(2,1)S(1)}) custom-call(bf16[27648,512]{1,0:T(8,128)(2,1)} %orb_ref.1, bf16[2048,512]{1,0:T(8,128)(2,1)S(1)} %bitcast.9, bf16[32,2048]{1,0:T(8,128)(2,1)S(1)} %bitcast.11, f32[4,32,1536]{2,1,0:T(8,128)S(1)} %get-tuple-element.11.early_ref), custom_call_target="tpu_custom_call" | custom-call | tf_op jit(solution)/shard_map/pair_fit_send/pallas_call | solution.py:647
  147.8 0.0 copy-start
  147.8 1.5 copy-done
  149.3 73.1 %solve_project.1 = f32[64,32]{1,0:T(8,128)} custom-call(bf16[96,96,128]{2,1,0:T(8,128)(2,1)} %bitcast.8, bf16[128,256]{1,0:T(8,128)(2,1)} %constant.26.clone.tz_ref, bf16[96,192]{1,0:T(8,128)(2,1)} %constant.27.clone.ty_ref, bf16[96,192]{1,0:T(8,128)(2,1)} %constant.28.clone.tyi_ref, bf16[128,128]{1,0:T(8,128)(2,1)} %constant.29.clone.tzi_ref, ...), custom_call_target="tpu_custom_call" | custom-call | tf_op jit(solution)/shard_map/solve_project/pallas_call | solution.py:913
  222.3 1.4 copy.9
Async XLA Ops:
  0.0 12.8 %copy-start.1 = (bf16[2048,32]{0,1:T(8,128)(2,1)S(1)}, bf16[2048,32]{0,1:T(8,128)(2,1)}, u32[]{:S(2)}) copy-start(bf16[2048,32]{0,1:T(8,128)(2,1)} %param.8) | copy-start | bytes 393220
  1.0 0.7 copy-start.2
  147.8 1.5 copy-start

commit v5 on v4

--- a/solution.py
+++ b/solution.py
@@ -505,7 +505,8 @@
 LINES = 16
 SPAN = LINES * NG
 TAKE = 512
-JOIN = 3
+JOIN = NG // LINES
+TAIL = (3, 5)
 EARLY = 4
 
 
@@ -599,20 +600,19 @@
     for first in range(TAKE, npoints // 2, TAKE):
         multiply(first)
 
-    @pl.when(block == EARLY)
+    @pl.when(block == EARLY + 1)
     def _():
         wait_greeted(count)
-        send(0, 0, tall)
 
     @pl.when((block > EARLY) & (lax.rem(block, JOIN) == 0))
     def _():
         send(block // JOIN - 1, 0, tall)
 
-    for late in range(JOIN - 1):
-
-        @pl.when(block == blocks - JOIN + 1 + late)
-        def _(late=late):
-            send(groups - 1, late * LINES, LINES)
+    for start, stop in zip((0,) + TAIL, TAIL):
+
+        @pl.when(block == blocks - JOIN + stop)
+        def _(start=start, stop=stop):
+            send(groups - 1, start * LINES, (stop - start) * LINES)
 
     for first in range(npoints // 2, npoints, TAKE):
         multiply(first)
@@ -623,7 +623,7 @@
     @pl.when(block == blocks - 1)
     def _():
         arrange(block)
-        send(groups - 1, (JOIN - 1) * LINES, LINES)
+        send(groups - 1, TAIL[-1] * LINES, (JOIN - TAIL[-1]) * LINES)
 
         def receive(step, carry):
             source = lax.rem(me + count - step, count)
@@ -678,7 +678,8 @@
 
 GROUP = 24
 HALF = 64
-PIECE = NG * NG // LANES // 3
+THIRDS = 3
+PIECE = NG * NG // LANES // THIRDS
 RING = EARLY
 
 
@@ -769,15 +770,17 @@
     lax.fori_loop(0, NG // GROUP, middle, 0)
     wait_greeted(count)
 
-    def own(piece):
-        return pltpu.make_async_copy(pot.at[piece, me], land.at[piece, me], own_sem.at[piece])
-
-    def send_piece(piece):
+    whole = (planes - 1) * THIRDS
+
+    def own(part, piece):
+        return pltpu.make_async_copy(pot.at[part, me], land.at[part, me], own_sem.at[piece])
+
+    def send_pieces(part, piece):
         def body(step, carry):
             peer = lax.rem(me + step, count)
             pltpu.make_async_remote_copy(
-                src_ref=pot.at[piece, peer],
-                dst_ref=land.at[piece, me],
+                src_ref=pot.at[part, peer],
+                dst_ref=land.at[part, me],
                 send_sem=send_sem.at[piece],
                 recv_sem=recv_sem.at[piece],
                 device_id=place(peer),
@@ -785,8 +788,17 @@
             ).start()
             return carry
 
-        own(piece).start()
-        lax.fori_loop(1, count, body, 0)
+        own(part, piece).start()
+        lax.fori_loop(1, count, body, 0, unroll=True)
+
+    def arrive(part, piece):
+        own(part, piece).wait()
+        others = land.at[part, pl.ds(0, count - 1)]
+        pltpu.make_async_copy(others, others, recv_sem.at[piece]).wait()
+
+    def leave(part, piece):
+        sent = pot.at[part, pl.ds(0, count - 1)]
+        pltpu.make_async_copy(sent, sent, send_sem.at[piece]).wait()
 
     quarter = NG // 4
     spot = lane[:quarter]
@@ -806,17 +818,30 @@
             dense[pl.ds(base + 2, quarter, stride=3), :] = jnp.where(spot < 32, y2, y3)
             for m in range(3):
                 pot[local * 3 + m, k] = dense[base + m * PIECE : base + (m + 1) * PIECE, :].astype(bf)
-        for m in range(3):
-            send_piece(local * 3 + m)
+
+        @pl.when(local < planes - 1)
+        def _():
+            send_pieces(pl.ds(local * THIRDS, THIRDS), local * THIRDS)
+
+        @pl.when(local == planes - 1)
+        def _():
+            for m in range(THIRDS):
+                send_pieces(pl.ds(whole + m, 1), whole + m)
+
         return carry
 
     lax.fori_loop(0, planes, backward, 0)
     total[...] = jnp.zeros_like(total)
 
     def work(piece, carry):
-        own(piece).wait()
-        others = land.at[piece, pl.ds(0, count - 1)]
-        pltpu.make_async_copy(others, others, recv_sem.at[piece]).wait()
+        @pl.when((piece < whole) & (lax.rem(piece, THIRDS) == 0))
+        def _():
+            arrive(pl.ds(piece, THIRDS), piece)
+
+        @pl.when(piece >= whole)
+        def _():
+            arrive(pl.ds(piece, 1), piece)
+
         wide[...] = land[piece].astype(f32).reshape(cols * PIECE, LANES)
         for half in range(per_piece):
             block = piece * per_piece + half
@@ -864,12 +889,10 @@
     lax.fori_loop(1, count, part_start, 0)
     held[me] = parts[me]
 
-    def drain_piece(piece, carry):
-        sent = pot.at[piece, pl.ds(0, count - 1)]
-        pltpu.make_async_copy(sent, sent, send_sem.at[piece]).wait()
-        return carry
-
-    lax.fori_loop(0, pieces, drain_piece, 0)
+    for local in range(planes - 1):
+        leave(pl.ds(local * THIRDS, THIRDS), local * THIRDS)
+    for m in range(THIRDS):
+        leave(pl.ds(whole + m, 1), whole + m)
 
     def part_receive(step, carry):
         source = lax.rem(me + count - step, count)
@@ -949,8 +972,8 @@
         cols == count
         and rows % (NG * NG) == 0
         and NG % (rows // (NG * NG)) == 0
-        and blocks >= EARLY + 2 * JOIN
-        and EARLY > JOIN
+        and blocks >= 3 * JOIN
+        and EARLY + 1 < JOIN
         and npoints % (count * ROWS) == 0
         and NG // LINES % JOIN == 0
         and npoints % TAKE == 0

time: 224 us -> 228 us (1.018)
  Pallas kernels: 219 us -> 222 us
    pallas_call x1, Pallas kernels: 73.1 us -> 78.4 us  [solve_and_project(): pl.pallas_call(solve_project_kernel, out_shape=jax.ShapeDtypeStruct((npoi...]
where the time goes in v5:
time: 228 us; the launch traced here: 227 us
  Pallas kernels  222 us (97%)
  local copies, waits for them, and re-layouts  3.69 us (2%)
    pallas_call x1, Pallas kernels, pair_and_fit(): pl.pallas_call(pair_fit_kernel, grid=(blocks,), in_specs=[pl.BlockSpec((S...  79.3 us
    pallas_call x1, Pallas kernels, solve_and_project(): pl.pallas_call(solve_project_kernel, out_shape=jax.ShapeDtypeStruct((npoi...  78.4 us
    pallas_call x1, Pallas kernels, share_rows(): pl.pallas_call(body, out_shape=out_shape, in_specs=in_specs, out_specs=ou...  54.5 us
    pallas_call x1, Pallas kernels, pick_rows(): pl.pallas_call(pick_kernel, out_shape=jax.ShapeDtypeStruct((npoints, norb...  10.2 us

profile of v5, /device:TPU:0, one launch (start us, length us, event | category | flops | bytes accessed | tf_op | source)
XLA Modules:
  0.0 227.1 jit_solution(3369021553285663512)
XLA Ops:
  0.0 0.0 copy-start.1
  0.0 0.7 and_convert_fusion
  0.7 0.1 reshape.23
  0.8 0.1 reduce_max.9.flags_ref
  1.0 0.0 copy-start.2
  1.0 0.7 copy-done.2
  1.7 10.2 %pick_rows.1 = bf16[2048,512]{1,0:T(8,128)(2,1)S(1)} custom-call(s32[2048]{0:T(1024)S(1)} %copy-done.2, s32[256]{0:T(256)S(1)} %reduce_max.9.flags_ref, s32[1]{0:T(128)} %bitcast.offset_ref, bf16[3456,8,512]{2,1,0:T(8,128)(2,1)} %bitcast.12), custom_call_target="tpu_custom_call" | custom-call | tf_op jit(solution)/shard_map/pick_rows/pallas_call | solution.py:435
  11.9 0.0 copy-done.1
  11.9 54.5 %share_rows.1 = (bf16[4,2,4,4,16,512]{5,4,3,2,1,0:T(8,128)(2,1)S(1)}, bf16[4,2048,1536]{2,1,0:T(8,128)(2,1)}, f32[4,32,1536]{2,1,0:T(8,128)S(1)}) custom-call(bf16[4,2,4,4,16,512]{5,4,3,2,1,0:T(8,128)(2,1)S(1)} %bitcast.7, bf16[32,2048]{1,0:T(8,128)(2,1)S(1)} %bitcast.10, bf16[18,1536,512]{2,1,0:T(8,128)(2,1)} %bitcast.13), custom_call_target="tpu_custom_call" | custom-call | tf_op jit(solution)/shard_map/share_rows/pallas_call | solution.py:356
  66.5 79.3 %pair_fit_send.1 = (bf16[14,2048,1536]{2,1,0:T(8,128)(2,1)}, bf16[32,3,96,128]{3,2,1,0:T(8,128)(2,1)S(1)}) custom-call(bf16[27648,512]{1,0:T(8,128)(2,1)} %orb_ref.1, bf16[2048,512]{1,0:T(8,128)(2,1)S(1)} %bitcast.9, bf16[32,2048]{1,0:T(8,128)(2,1)S(1)} %bitcast.11, f32[4,32,1536]{2,1,0:T(8,128)S(1)} %get-tuple-element.11.early_ref), custom_call_target="tpu_custom_call" | custom-call | tf_op jit(solution)/shard_map/pair_fit_send/pallas_call | solution.py:647
  145.8 0.0 copy-start
  145.8 1.5 copy-done
  147.3 78.4 %solve_project.1 = f32[64,32]{1,0:T(8,128)} custom-call(bf16[96,96,128]{2,1,0:T(8,128)(2,1)} %bitcast.8, bf16[128,256]{1,0:T(8,128)(2,1)} %constant.26.clone.tz_ref, bf16[96,192]{1,0:T(8,128)(2,1)} %constant.27.clone.ty_ref, bf16[96,192]{1,0:T(8,128)(2,1)} %constant.28.clone.tyi_ref, bf16[128,128]{1,0:T(8,128)(2,1)} %constant.29.clone.tzi_ref, ...), custom_call_target="tpu_custom_call" | custom-call | tf_op jit(solution)/shard_map/solve_project/pallas_call | solution.py:936
  225.6 1.4 copy.9
Async XLA Ops:
  0.0 11.9 %copy-start.1 = (bf16[2048,32]{0,1:T(8,128)(2,1)S(1)}, bf16[2048,32]{0,1:T(8,128)(2,1)}, u32[]{:S(2)}) copy-start(bf16[2048,32]{0,1:T(8,128)(2,1)} %param.8) | copy-start | bytes 393220
  1.0 0.7 copy-start.2
  145.8 1.5 copy-start

commit v6 on v4

--- a/solution.py
+++ b/solution.py
@@ -481,6 +481,10 @@
     return count, me, place
 
 
+def shift_of(step, count):
+    return lax.rem(step, 2) * (count // 2) + step // 2
+
+
 def greet_all(count, me, place):
     barrier = pltpu.get_barrier_semaphore()
 
@@ -529,7 +533,7 @@
         target = field_ref.at[me, group * JOIN // per_plane, pl.ds(start, lines)]
 
         def body(step, carry):
-            peer = lax.rem(me + step, count)
+            peer = lax.rem(me + shift_of(step, count), count)
             pltpu.make_async_remote_copy(
                 src_ref=out_buf.at[slot, peer, pl.ds(begin, lines)],
                 dst_ref=target,
@@ -774,7 +778,7 @@
 
     def send_piece(piece):
         def body(step, carry):
-            peer = lax.rem(me + step, count)
+            peer = lax.rem(me + shift_of(step, count), count)
             pltpu.make_async_remote_copy(
                 src_ref=pot.at[piece, peer],
                 dst_ref=land.at[piece, me],
@@ -858,7 +862,8 @@
         )
 
     def part_start(step, carry):
-        part_copy(step, lax.rem(me + step, count), me).start()
+        shift = shift_of(step, count)
+        part_copy(shift, lax.rem(me + shift, count), me).start()
         return carry
 
     lax.fori_loop(1, count, part_start, 0)
@@ -947,6 +952,7 @@
     blocks = rows // SPAN
     return (
         cols == count
+        and count % 2 == 0
         and rows % (NG * NG) == 0
         and NG % (rows // (NG * NG)) == 0
         and blocks >= EARLY + 2 * JOIN

time: 224 us -> 227 us (1.013)
  Pallas kernels: 219 us -> 222 us
    pallas_call x1, Pallas kernels: 73.1 us -> 75.9 us  [solve_and_project(): pl.pallas_call(solve_project_kernel, out_shape=jax.ShapeDtypeStruct((npoi...]
where the time goes in v6:
time: 227 us; the launch traced here: 226 us
  Pallas kernels  222 us (98%)
  local copies, waits for them, and re-layouts  3.69 us (2%)
    pallas_call x1, Pallas kernels, pair_and_fit(): pl.pallas_call(pair_fit_kernel, grid=(blocks,), in_specs=[pl.BlockSpec((S...  80.6 us
    pallas_call x1, Pallas kernels, solve_and_project(): pl.pallas_call(solve_project_kernel, out_shape=jax.ShapeDtypeStruct((npoi...  75.9 us
    pallas_call x1, Pallas kernels, share_rows(): pl.pallas_call(body, out_shape=out_shape, in_specs=in_specs, out_specs=ou...  53.3 us
    pallas_call x1, Pallas kernels, pick_rows(): pl.pallas_call(pick_kernel, out_shape=jax.ShapeDtypeStruct((npoints, norb...  11.7 us

profile of v6, /device:TPU:0, one launch (start us, length us, event | category | flops | bytes accessed | tf_op | source)
XLA Modules:
  0.0 226.2 jit_solution(8317164872097524967)
XLA Ops:
  0.0 0.0 copy-start.1
  0.0 0.7 and_convert_fusion
  0.7 0.1 reshape.23
  0.8 0.1 reduce_max.9.flags_ref
  1.0 0.0 copy-start.2
  1.0 0.7 copy-done.2
  1.7 11.7 %pick_rows.1 = bf16[2048,512]{1,0:T(8,128)(2,1)S(1)} custom-call(s32[2048]{0:T(1024)S(1)} %copy-done.2, s32[256]{0:T(256)S(1)} %reduce_max.9.flags_ref, s32[1]{0:T(128)} %bitcast.offset_ref, bf16[3456,8,512]{2,1,0:T(8,128)(2,1)} %bitcast.12), custom_call_target="tpu_custom_call" | custom-call | tf_op jit(solution)/shard_map/pick_rows/pallas_call | solution.py:435
  13.4 0.0 copy-done.1
  13.4 53.3 %share_rows.1 = (bf16[4,2,4,4,16,512]{5,4,3,2,1,0:T(8,128)(2,1)S(1)}, bf16[4,2048,1536]{2,1,0:T(8,128)(2,1)}, f32[4,32,1536]{2,1,0:T(8,128)S(1)}) custom-call(bf16[4,2,4,4,16,512]{5,4,3,2,1,0:T(8,128)(2,1)S(1)} %bitcast.7, bf16[32,2048]{1,0:T(8,128)(2,1)S(1)} %bitcast.10, bf16[18,1536,512]{2,1,0:T(8,128)(2,1)} %bitcast.13), custom_call_target="tpu_custom_call" | custom-call | tf_op jit(solution)/shard_map/share_rows/pallas_call | solution.py:356
  66.7 80.6 %pair_fit_send.1 = (bf16[14,2048,1536]{2,1,0:T(8,128)(2,1)}, bf16[32,3,96,128]{3,2,1,0:T(8,128)(2,1)S(1)}) custom-call(bf16[27648,512]{1,0:T(8,128)(2,1)} %orb_ref.1, bf16[2048,512]{1,0:T(8,128)(2,1)S(1)} %bitcast.9, bf16[32,2048]{1,0:T(8,128)(2,1)S(1)} %bitcast.11, f32[4,32,1536]{2,1,0:T(8,128)S(1)} %get-tuple-element.11.early_ref), custom_call_target="tpu_custom_call" | custom-call | tf_op jit(solution)/shard_map/pair_fit_send/pallas_call | solution.py:651
  147.4 0.0 copy-start
  147.4 1.5 copy-done
  148.8 75.9 %solve_project.1 = f32[64,32]{1,0:T(8,128)} custom-call(bf16[96,96,128]{2,1,0:T(8,128)(2,1)} %bitcast.8, bf16[128,256]{1,0:T(8,128)(2,1)} %constant.26.clone.tz_ref, bf16[96,192]{1,0:T(8,128)(2,1)} %constant.27.clone.ty_ref, bf16[96,192]{1,0:T(8,128)(2,1)} %constant.28.clone.tyi_ref, bf16[128,128]{1,0:T(8,128)(2,1)} %constant.29.clone.tzi_ref, ...), custom_call_target="tpu_custom_call" | custom-call | tf_op jit(solution)/shard_map/solve_project/pallas_call | solution.py:918
  224.7 1.4 copy.9
Async XLA Ops:
  0.0 13.4 %copy-start.1 = (bf16[2048,32]{0,1:T(8,128)(2,1)S(1)}, bf16[2048,32]{0,1:T(8,128)(2,1)}, u32[]{:S(2)}) copy-start(bf16[2048,32]{0,1:T(8,128)(2,1)} %param.8) | copy-start | bytes 393220
  1.0 0.7 copy-start.2
  147.4 1.5 copy-start

commit v7 on v4

--- a/solution.py
+++ b/solution.py
@@ -150,9 +150,9 @@
 
 def share_kernel(chunks, early, refs):
     if early:
-        x_ref, panel_ref, orb_ref, o_ref, early_ref, fit_ref = refs[:6]
-        orbs, pairs, orb_sem, pair_sem = refs[-4:]
-        near, wide, far, sum1, sum2, sum3, sends, recvs, own_sem = refs[6:-4]
+        x_ref, panel_ref, orb_ref, o_ref, early_ref, lines_ref, fit_ref = refs[:7]
+        orbs, pairs, fit_rows, orb_sem, pair_sem = refs[-5:]
+        near, wide, far, sum1, sum2, sum3, sends, recvs, own_sem = refs[7:-5]
     else:
         x_ref, o_ref, near, wide, far, sum1, sum2, sum3, sends, recvs, own_sem = refs
     bf = jnp.bfloat16
@@ -289,8 +289,12 @@
             keep(tick - 6).start()
     if early:
 
+        fit_ref[...] = jnp.zeros_like(fit_ref)
+
         def fit(e, carry):
-            fit_ref[e] = lax.dot_general(
+            begin = pl.multiple_of(jnp.maximum(e - 1, 0) * LINES, LINES)
+            lines_ref[:, pl.ds(begin, LINES), :] = split_lines(fit_ref, fit_rows)
+            fit_ref[...] = lax.dot_general(
                 panel_ref[...], pairs[e], NN, preferred_element_type=f32
             )
             return carry
@@ -338,14 +342,16 @@
         cols = panel.shape[0]
         args += [panel, orbitals.reshape(-1, SPAN, norb)]
         in_specs += [vmem_spec, any_spec]
-        out_specs += [any_spec, vmem_spec]
+        out_specs += [any_spec, vmem_spec, vmem_spec]
         out_shape += [
             jax.ShapeDtypeStruct((early, npoints, SPAN), bf),
-            jax.ShapeDtypeStruct((early, cols, SPAN), jnp.float32),
+            jax.ShapeDtypeStruct((cols, (early - 1) * LINES, LANES), bf),
+            jax.ShapeDtypeStruct((cols, SPAN), jnp.float32),
         ]
         scratch += [
             pltpu.VMEM((early, SPAN, norb), bf),
             pltpu.VMEM((early, npoints, SPAN), bf),
+            pltpu.VMEM((cols * LINES, LANES), jnp.float32),
             pltpu.SemaphoreType.DMA(()),
             pltpu.SemaphoreType.DMA((chunks,)),
         ]
@@ -365,7 +371,7 @@
         name="share_rows",
     )(*args)
     rows = outs[0].reshape(npoints, norb)
-    return (rows, outs[1], outs[2]) if early else rows
+    return (rows, *outs[1:]) if early else rows
 
 
 OCTET = 8
@@ -509,8 +515,23 @@
 EARLY = 4
 
 
+def split_lines(fit_ref, fit_rows):
+    cols = fit_ref.shape[0]
+    for line in range(LINES):
+        begin = line * NG
+        low = begin // LANES * LANES
+        turn = begin - low
+        wide = fit_ref[:, low : min(low + 2 * LANES, SPAN)]
+        if wide.shape[1] == LANES:
+            wide = jnp.concatenate([wide, wide], axis=1)
+        if turn:
+            wide = pltpu.roll(wide, 2 * LANES - turn, 1)
+        fit_rows[pl.ds(line, cols, stride=LINES), :] = wide[:, :LANES]
+    return fit_rows[...].astype(jnp.bfloat16).reshape(cols, LINES, LANES)
+
+
 def pair_fit_kernel(
-    orb_ref, rows_ref, panel_ref, early_ref, pair_ref, field_ref, fit_buf, fit_rows, out_buf,
+    orb_ref, rows_ref, panel_ref, early_ref, last_ref, pair_ref, field_ref, fit_buf, fit_rows, out_buf,
     send_sem, recv_sem, own_sem,
 ):
     bf = jnp.bfloat16
@@ -523,15 +544,16 @@
     groups = blocks // JOIN
     tall = JOIN * LINES
 
-    def send(group, begin, lines):
+    def send(group, begin, lines, source=None):
         slot = lax.rem(group, 2)
+        source = out_buf.at[slot] if source is None else source
         start = pl.multiple_of(lax.rem(group * JOIN, per_plane) * LINES + begin, LINES)
         target = field_ref.at[me, group * JOIN // per_plane, pl.ds(start, lines)]
 
         def body(step, carry):
             peer = lax.rem(me + step, count)
             pltpu.make_async_remote_copy(
-                src_ref=out_buf.at[slot, peer, pl.ds(begin, lines)],
+                src_ref=source.at[peer, pl.ds(begin, lines)],
                 dst_ref=target,
                 send_sem=send_sem.at[slot],
                 recv_sem=recv_sem.at[me],
@@ -541,7 +563,7 @@
             return carry
 
         pltpu.make_async_copy(
-            out_buf.at[slot, me, pl.ds(begin, lines)], target, own_sem.at[slot]
+            source.at[me, pl.ds(begin, lines)], target, own_sem.at[slot]
         ).start()
         lax.fori_loop(1, count, body, 0, unroll=True)
 
@@ -569,30 +591,14 @@
         pair_ref[0, first : first + TAKE, :] = (part * part).astype(bf)
 
     def arrange(index):
-        for line in range(LINES):
-            begin = line * NG
-            low = begin // LANES * LANES
-            turn = begin - low
-            wide = fit_buf[:, low : min(low + 2 * LANES, SPAN)]
-            if wide.shape[1] == LANES:
-                wide = jnp.concatenate([wide, wide], axis=1)
-            if turn:
-                wide = pltpu.roll(wide, 2 * LANES - turn, 1)
-            fit_rows[pl.ds(line, cols, stride=LINES), :] = wide[:, :LANES]
-        slot = index // JOIN % 2
-        begin = index % JOIN * LINES
-        if not isinstance(index, int):
-            begin = pl.multiple_of(begin, LINES)
-        out_buf[slot, :, pl.ds(begin, LINES), :] = (
-            fit_rows[...].astype(bf).reshape(cols, LINES, LANES)
+        begin = pl.multiple_of(lax.rem(index, JOIN) * LINES, LINES)
+        out_buf[lax.rem(index // JOIN, 2), :, pl.ds(begin, LINES), :] = split_lines(
+            fit_buf, fit_rows
         )
 
     @pl.when(block == EARLY)
     def _():
-        for index in range(EARLY - 1):
-            fit_buf[...] = early_ref[index]
-            arrange(index)
-        fit_buf[...] = early_ref[EARLY - 1]
+        fit_buf[...] = last_ref[...]
 
     multiply(0)
     arrange(before)
@@ -602,7 +608,7 @@
     @pl.when(block == EARLY)
     def _():
         wait_greeted(count)
-        send(0, 0, tall)
+        send(0, 0, tall, early_ref)
 
     @pl.when((block > EARLY) & (lax.rem(block, JOIN) == 0))
     def _():
@@ -636,7 +642,7 @@
         drain(groups - 1)
 
 
-def pair_and_fit(orbitals, point_rows, panel, early_fit):
+def pair_and_fit(orbitals, point_rows, panel, early_fit, last_fit):
     bf = jnp.bfloat16
     rows, norb = orbitals.shape
     npoints = point_rows.shape[0]
@@ -651,11 +657,12 @@
             pl.BlockSpec((SPAN, norb), lambda i: (i + EARLY, 0)),
             pl.BlockSpec((npoints, norb), lambda i: (0, 0)),
             pl.BlockSpec((cols, npoints), lambda i: (0, 0)),
-            pl.BlockSpec((EARLY, cols, SPAN), lambda i: (0, 0, 0)),
+            pl.BlockSpec((cols, JOIN * LINES, LANES), lambda i: (0, 0, 0)),
+            pl.BlockSpec((cols, SPAN), lambda i: (0, 0)),
         ],
         out_specs=[
             pl.BlockSpec((1, npoints, SPAN), lambda i: (i, 0, 0)),
-            pl.BlockSpec(memory_space=pl.ANY),
+            pl.BlockSpec(memory_space=pltpu.HBM),
         ],
         out_shape=[
             jax.ShapeDtypeStruct((blocks, npoints, SPAN), bf),
@@ -670,10 +677,10 @@
             pltpu.SemaphoreType.DMA((2,)),
         ],
         compiler_params=pltpu.CompilerParams(
-            collective_id=1, has_side_effects=True, vmem_limit_bytes=36 << 20
+            collective_id=1, has_side_effects=True, vmem_limit_bytes=50 << 20
         ),
         name="pair_fit_send",
-    )(orbitals, point_rows, panel, early_fit)
+    )(orbitals, point_rows, panel, early_fit, last_fit)
 
 
 GROUP = 24
@@ -879,7 +886,7 @@
     lax.fori_loop(1, count, part_receive, 0)
     summed = jnp.sum(held[...], axis=0)
     pile = jnp.concatenate([summed, pltpu.roll(summed, share, 1)], axis=0)
-    o_ref[...] = pile.T[:share, :]
+    o_ref[...] = pile[:, :share]
 
     def part_drain(step, carry):
         part_copy(step, lax.rem(me + step, count), me).wait_send()
@@ -912,7 +919,7 @@
     vmem_spec = pl.BlockSpec(memory_space=pltpu.VMEM)
     return pl.pallas_call(
         solve_project_kernel,
-        out_shape=jax.ShapeDtypeStruct((npoints // count, cols), f32),
+        out_shape=jax.ShapeDtypeStruct((cols, npoints // count), f32),
         in_specs=[any_spec] + [vmem_spec] * 4 + [any_spec] * 2,
         out_specs=vmem_spec,
         scratch_shapes=[
@@ -940,7 +947,7 @@
             collective_id=2, has_side_effects=True, vmem_limit_bytes=54 << 20
         ),
         name="solve_project",
-    )(field.reshape(NG, NG, LANES), tz, ty, tyi, tzi, early, pair)
+    )(field.reshape(NG, NG, LANES), tz, ty, tyi, tzi, early, pair).T
 
 
 def fits_planes(rows, npoints, cols, count):
@@ -950,7 +957,7 @@
         and rows % (NG * NG) == 0
         and NG % (rows // (NG * NG)) == 0
         and blocks >= EARLY + 2 * JOIN
-        and EARLY > JOIN
+        and EARLY == JOIN + 1
         and npoints % (count * ROWS) == 0
         and NG // LINES % JOIN == 0
         and npoints % TAKE == 0
@@ -969,8 +976,8 @@
     cols = inverse_panel.shape[1]
     if fits_planes(row_count, npoints, cols, grid_count * vec_count):
         panel = inverse_panel.T
-        point_rows, early, early_fit = share_rows(picked, grid_count, vec_count, panel, orbitals)
-        pair, field = pair_and_fit(orbitals, point_rows, panel, early_fit)
+        point_rows, early, *fits = share_rows(picked, grid_count, vec_count, panel, orbitals)
+        pair, field = pair_and_fit(orbitals, point_rows, panel, *fits)
         return solve_and_project(field, early, pair, grid_count * vec_count)
     point_rows = share_rows(picked, grid_count, vec_count)
 

time: 224 us -> 223 us (level)
  no operation moved by 1% of the time
where the time goes in v7:
time: 223 us; the launch traced here: 222 us
  Pallas kernels  219 us (98%)
    pallas_call x1, Pallas kernels, pair_and_fit(): pl.pallas_call(pair_fit_kernel, grid=(blocks,), in_specs=[pl.BlockSpec((S...  79.9 us
    pallas_call x1, Pallas kernels, solve_and_project(): pl.pallas_call(solve_project_kernel, out_shape=jax.ShapeDtypeStruct((cols...  73.8 us
    pallas_call x1, Pallas kernels, share_rows(): pl.pallas_call(body, out_shape=out_shape, in_specs=in_specs, out_specs=ou...  55 us
    pallas_call x1, Pallas kernels, pick_rows(): pl.pallas_call(pick_kernel, out_shape=jax.ShapeDtypeStruct((npoints, norb...  10.7 us

profile of v7, /device:TPU:0, one launch (start us, length us, event | category | flops | bytes accessed | tf_op | source)
XLA Modules:
  0.0 222.4 jit_solution(3185491228999769150)
XLA Ops:
  0.0 0.0 copy-start
  0.0 0.7 and_convert_fusion
  0.7 0.1 reshape.23
  0.8 0.1 reduce_max.9.flags_ref
  1.0 0.0 copy-start.1
  1.0 0.7 copy-done.1
  1.7 10.7 %pick_rows.1 = bf16[2048,512]{1,0:T(8,128)(2,1)S(1)} custom-call(s32[2048]{0:T(1024)S(1)} %copy-done.1, s32[256]{0:T(256)S(1)} %reduce_max.9.flags_ref, s32[1]{0:T(128)} %bitcast.offset_ref, bf16[3456,8,512]{2,1,0:T(8,128)(2,1)} %bitcast.12), custom_call_target="tpu_custom_call" | custom-call | tf_op jit(solution)/shard_map/pick_rows/pallas_call | solution.py:441
  12.4 0.0 copy-done
  12.4 55.0 %share_rows.1 = (bf16[4,2,4,4,16,512]{5,4,3,2,1,0:T(8,128)(2,1)S(1)}, bf16[4,2048,1536]{2,1,0:T(8,128)(2,1)}, bf16[32,48,128]{2,1,0:T(8,128)(2,1)S(1)}, f32[32,1536]{1,0:T(8,128)S(1)}) custom-call(bf16[4,2,4,4,16,512]{5,4,3,2,1,0:T(8,128)(2,1)S(1)} %bitcast.8, bf16[32,2048]{1,0:T(8,128)(2,1)S(1)} %bitcast.10, bf16[18,1536,512]{2,1,0:T(8,128)(2,1)} %bitcast.13), custom_call_target="tpu_custom_call" | custom-call | tf_op jit(solution)/shard_map/share_rows/pallas_call | solution.py:362
  67.5 79.9 %pair_fit_send.1 = (bf16[14,2048,1536]{2,1,0:T(8,128)(2,1)}, bf16[32,3,96,128]{3,2,1,0:T(8,128)(2,1)}) custom-call(bf16[27648,512]{1,0:T(8,128)(2,1)} %orb_ref.1, bf16[2048,512]{1,0:T(8,128)(2,1)S(1)} %bitcast.9, bf16[32,2048]{1,0:T(8,128)(2,1)S(1)} %bitcast.11, bf16[32,48,128]{2,1,0:T(8,128)(2,1)S(1)} %get-tuple-element.12.early_ref, ...), custom_call_target="tpu_custom_call" | custom-call | tf_op jit(solution)/shard_map/pair_fit_send/pallas_call | solution.py:653
  147.3 73.8 %solve_project.1 = f32[32,64]{1,0:T(8,128)} custom-call(bf16[96,96,128]{2,1,0:T(8,128)(2,1)} %bitcast.14, bf16[128,256]{1,0:T(8,128)(2,1)} %constant.26.clone.tz_ref, bf16[96,192]{1,0:T(8,128)(2,1)} %constant.27.clone.ty_ref, bf16[96,192]{1,0:T(8,128)(2,1)} %constant.28.clone.tyi_ref, bf16[128,128]{1,0:T(8,128)(2,1)} %constant.29.clone.tzi_ref, ...), custom_call_target="tpu_custom_call" | custom-call | tf_op jit(solution)/shard_map/solve_project/pallas_call | solution.py:920
  221.1 1.3 copy.9
Async XLA Ops:
  0.0 12.4 %copy-start = (bf16[2048,32]{0,1:T(8,128)(2,1)S(1)}, bf16[2048,32]{0,1:T(8,128)(2,1)}, u32[]{:S(2)}) copy-start(bf16[2048,32]{0,1:T(8,128)(2,1)} %param.8) | copy-start | bytes 393220
  1.0 0.7 copy-start.1

commit v8 on v7

--- a/solution.py
+++ b/solution.py
@@ -511,7 +511,8 @@
 LINES = 16
 SPAN = LINES * NG
 TAKE = 512
-JOIN = 3
+JOIN = NG // LINES
+TAIL = (3, 4, 5)
 EARLY = 4
 
 
@@ -544,16 +545,15 @@
     groups = blocks // JOIN
     tall = JOIN * LINES
 
-    def send(group, begin, lines, source=None):
+    def send(group, begin, lines):
         slot = lax.rem(group, 2)
-        source = out_buf.at[slot] if source is None else source
         start = pl.multiple_of(lax.rem(group * JOIN, per_plane) * LINES + begin, LINES)
         target = field_ref.at[me, group * JOIN // per_plane, pl.ds(start, lines)]
 
         def body(step, carry):
             peer = lax.rem(me + step, count)
             pltpu.make_async_remote_copy(
-                src_ref=source.at[peer, pl.ds(begin, lines)],
+                src_ref=out_buf.at[slot, peer, pl.ds(begin, lines)],
                 dst_ref=target,
                 send_sem=send_sem.at[slot],
                 recv_sem=recv_sem.at[me],
@@ -563,7 +563,7 @@
             return carry
 
         pltpu.make_async_copy(
-            source.at[me, pl.ds(begin, lines)], target, own_sem.at[slot]
+            out_buf.at[slot, me, pl.ds(begin, lines)], target, own_sem.at[slot]
         ).start()
         lax.fori_loop(1, count, body, 0, unroll=True)
 
@@ -599,26 +599,26 @@
     @pl.when(block == EARLY)
     def _():
         fit_buf[...] = last_ref[...]
+        out_buf[0, :, : (EARLY - 1) * LINES, :] = early_ref[...]
 
     multiply(0)
     arrange(before)
     for first in range(TAKE, npoints // 2, TAKE):
         multiply(first)
 
-    @pl.when(block == EARLY)
+    @pl.when(block == EARLY + 1)
     def _():
         wait_greeted(count)
-        send(0, 0, tall, early_ref)
 
     @pl.when((block > EARLY) & (lax.rem(block, JOIN) == 0))
     def _():
         send(block // JOIN - 1, 0, tall)
 
-    for late in range(JOIN - 1):
-
-        @pl.when(block == blocks - JOIN + 1 + late)
-        def _(late=late):
-            send(groups - 1, late * LINES, LINES)
+    for start, stop in zip((0,) + TAIL, TAIL):
+
+        @pl.when(block == blocks - JOIN + stop)
+        def _(start=start, stop=stop):
+            send(groups - 1, start * LINES, (stop - start) * LINES)
 
     for first in range(npoints // 2, npoints, TAKE):
         multiply(first)
@@ -629,7 +629,7 @@
     @pl.when(block == blocks - 1)
     def _():
         arrange(block)
-        send(groups - 1, (JOIN - 1) * LINES, LINES)
+        send(groups - 1, TAIL[-1] * LINES, (JOIN - TAIL[-1]) * LINES)
 
         def receive(step, carry):
             source = lax.rem(me + count - step, count)
@@ -657,7 +657,7 @@
             pl.BlockSpec((SPAN, norb), lambda i: (i + EARLY, 0)),
             pl.BlockSpec((npoints, norb), lambda i: (0, 0)),
             pl.BlockSpec((cols, npoints), lambda i: (0, 0)),
-            pl.BlockSpec((cols, JOIN * LINES, LANES), lambda i: (0, 0, 0)),
+            pl.BlockSpec((cols, (EARLY - 1) * LINES, LANES), lambda i: (0, 0, 0)),
             pl.BlockSpec((cols, SPAN), lambda i: (0, 0)),
         ],
         out_specs=[
@@ -685,7 +685,8 @@
 
 GROUP = 24
 HALF = 64
-PIECE = NG * NG // LANES // 3
+THIRDS = 3
+PIECE = NG * NG // LANES // THIRDS
 RING = EARLY
 
 
@@ -776,15 +777,17 @@
     lax.fori_loop(0, NG // GROUP, middle, 0)
     wait_greeted(count)
 
-    def own(piece):
-        return pltpu.make_async_copy(pot.at[piece, me], land.at[piece, me], own_sem.at[piece])
-
-    def send_piece(piece):
+    whole = (planes - 1) * THIRDS
+
+    def own(part, piece):
+        return pltpu.make_async_copy(pot.at[part, me], land.at[part, me], own_sem.at[piece])
+
+    def send_pieces(part, piece):
         def body(step, carry):
             peer = lax.rem(me + step, count)
             pltpu.make_async_remote_copy(
-                src_ref=pot.at[piece, peer],
-                dst_ref=land.at[piece, me],
+                src_ref=pot.at[part, peer],
+                dst_ref=land.at[part, me],
                 send_sem=send_sem.at[piece],
                 recv_sem=recv_sem.at[piece],
                 device_id=place(peer),
@@ -792,8 +795,17 @@
             ).start()
             return carry
 
-        own(piece).start()
-        lax.fori_loop(1, count, body, 0)
+        own(part, piece).start()
+        lax.fori_loop(1, count, body, 0, unroll=True)
+
+    def arrive(part, piece):
+        own(part, piece).wait()
+        others = land.at[part, pl.ds(0, count - 1)]
+        pltpu.make_async_copy(others, others, recv_sem.at[piece]).wait()
+
+    def leave(part, piece):
+        sent = pot.at[part, pl.ds(0, count - 1)]
+        pltpu.make_async_copy(sent, sent, send_sem.at[piece]).wait()
 
     quarter = NG // 4
     spot = lane[:quarter]
@@ -813,17 +825,33 @@
             dense[pl.ds(base + 2, quarter, stride=3), :] = jnp.where(spot < 32, y2, y3)
             for m in range(3):
                 pot[local * 3 + m, k] = dense[base + m * PIECE : base + (m + 1) * PIECE, :].astype(bf)
-        for m in range(3):
-            send_piece(local * 3 + m)
+        @pl.when(local < planes - 1)
+        def _():
+            send_pieces(pl.ds(local * THIRDS, 2), local * THIRDS)
+
+        @pl.when(local == planes - 1)
+        def _():
+            for m in range(THIRDS - 1):
+                send_pieces(pl.ds(whole + m, 1), whole + m)
+
+        last = local * THIRDS + 2
+        send_pieces(pl.ds(last, 1), last)
         return carry
 
     lax.fori_loop(0, planes, backward, 0)
     total[...] = jnp.zeros_like(total)
 
     def work(piece, carry):
-        own(piece).wait()
-        others = land.at[piece, pl.ds(0, count - 1)]
-        pltpu.make_async_copy(others, others, recv_sem.at[piece]).wait()
+        third = lax.rem(piece, THIRDS)
+
+        @pl.when((piece < whole) & (third == 0))
+        def _():
+            arrive(pl.ds(piece, 2), piece)
+
+        @pl.when((piece >= whole) | (third == 2))
+        def _():
+            arrive(pl.ds(piece, 1), piece)
+
         wide[...] = land[piece].astype(f32).reshape(cols * PIECE, LANES)
         for half in range(per_piece):
             block = piece * per_piece + half
@@ -871,12 +899,11 @@
     lax.fori_loop(1, count, part_start, 0)
     held[me] = parts[me]
 
-    def drain_piece(piece, carry):
-        sent = pot.at[piece, pl.ds(0, count - 1)]
-        pltpu.make_async_copy(sent, sent, send_sem.at[piece]).wait()
-        return carry
-
-    lax.fori_loop(0, pieces, drain_piece, 0)
+    for piece in range(pieces):
+        if piece >= whole or piece % THIRDS == 2:
+            leave(pl.ds(piece, 1), piece)
+        elif piece % THIRDS == 0:
+            leave(pl.ds(piece, 2), piece)
 
     def part_receive(step, carry):
         source = lax.rem(me + count - step, count)
@@ -956,8 +983,8 @@
         cols == count
         and rows % (NG * NG) == 0
         and NG % (rows // (NG * NG)) == 0
-        and blocks >= EARLY + 2 * JOIN
-        and EARLY == JOIN + 1
+        and blocks >= 3 * JOIN
+        and EARLY + 1 < JOIN
         and npoints % (count * ROWS) == 0
         and NG // LINES % JOIN == 0
         and npoints % TAKE == 0

time: 223 us -> 224 us (level)
    pallas_call x1, Pallas kernels: 73.8 us -> 76.3 us  [solve_and_project(): pl.pallas_call(solve_project_kernel, out_shape=jax.ShapeDtypeStruct((cols...]
where the time goes in v8:
time: 224 us
  Pallas kernels  221 us (99%)
    pallas_call x1, Pallas kernels, pair_and_fit(): pl.pallas_call(pair_fit_kernel, grid=(blocks,), in_specs=[pl.BlockSpec((S...  79.3 us
    pallas_call x1, Pallas kernels, solve_and_project(): pl.pallas_call(solve_project_kernel, out_shape=jax.ShapeDtypeStruct((cols...  76.3 us
    pallas_call x1, Pallas kernels, share_rows(): pl.pallas_call(body, out_shape=out_shape, in_specs=in_specs, out_specs=ou...  54.9 us
    pallas_call x1, Pallas kernels, pick_rows(): pl.pallas_call(pick_kernel, out_shape=jax.ShapeDtypeStruct((npoints, norb...  10.7 us

profile of v8, /device:TPU:0, one launch (start us, length us, event | category | flops | bytes accessed | tf_op | source)
XLA Modules:
  0.0 224.2 jit_solution(4786980470735460194)
XLA Ops:
  0.0 0.0 copy-start
  0.0 0.7 and_convert_fusion
  0.7 0.1 reshape.23
  0.8 0.1 reduce_max.9.flags_ref
  1.0 0.0 copy-start.1
  1.0 0.7 copy-done.1
  1.7 10.7 %pick_rows.1 = bf16[2048,512]{1,0:T(8,128)(2,1)S(1)} custom-call(s32[2048]{0:T(1024)S(1)} %copy-done.1, s32[256]{0:T(256)S(1)} %reduce_max.9.flags_ref, s32[1]{0:T(128)} %bitcast.offset_ref, bf16[3456,8,512]{2,1,0:T(8,128)(2,1)} %bitcast.12), custom_call_target="tpu_custom_call" | custom-call | tf_op jit(solution)/shard_map/pick_rows/pallas_call | solution.py:441
  12.3 0.0 copy-done
  12.4 54.9 %share_rows.1 = (bf16[4,2,4,4,16,512]{5,4,3,2,1,0:T(8,128)(2,1)S(1)}, bf16[4,2048,1536]{2,1,0:T(8,128)(2,1)}, bf16[32,48,128]{2,1,0:T(8,128)(2,1)S(1)}, f32[32,1536]{1,0:T(8,128)S(1)}) custom-call(bf16[4,2,4,4,16,512]{5,4,3,2,1,0:T(8,128)(2,1)S(1)} %bitcast.8, bf16[32,2048]{1,0:T(8,128)(2,1)S(1)} %bitcast.10, bf16[18,1536,512]{2,1,0:T(8,128)(2,1)} %bitcast.13), custom_call_target="tpu_custom_call" | custom-call | tf_op jit(solution)/shard_map/share_rows/pallas_call | solution.py:362
  67.3 79.3 %pair_fit_send.1 = (bf16[14,2048,1536]{2,1,0:T(8,128)(2,1)}, bf16[32,3,96,128]{3,2,1,0:T(8,128)(2,1)}) custom-call(bf16[27648,512]{1,0:T(8,128)(2,1)} %orb_ref.1, bf16[2048,512]{1,0:T(8,128)(2,1)S(1)} %bitcast.9, bf16[32,2048]{1,0:T(8,128)(2,1)S(1)} %bitcast.11, bf16[32,48,128]{2,1,0:T(8,128)(2,1)S(1)} %get-tuple-element.12.early_ref, ...), custom_call_target="tpu_custom_call" | custom-call | tf_op jit(solution)/shard_map/pair_fit_send/pallas_call | solution.py:653
  146.6 76.3 %solve_project.1 = f32[32,64]{1,0:T(8,128)} custom-call(bf16[96,96,128]{2,1,0:T(8,128)(2,1)} %bitcast.14, bf16[128,256]{1,0:T(8,128)(2,1)} %constant.26.clone.tz_ref, bf16[96,192]{1,0:T(8,128)(2,1)} %constant.27.clone.ty_ref, bf16[96,192]{1,0:T(8,128)(2,1)} %constant.28.clone.tyi_ref, bf16[128,128]{1,0:T(8,128)(2,1)} %constant.29.clone.tzi_ref, ...), custom_call_target="tpu_custom_call" | custom-call | tf_op jit(solution)/shard_map/solve_project/pallas_call | solution.py:947
  222.9 1.3 copy.9
Async XLA Ops:
  0.0 12.3 %copy-start = (bf16[2048,32]{0,1:T(8,128)(2,1)S(1)}, bf16[2048,32]{0,1:T(8,128)(2,1)}, u32[]{:S(2)}) copy-start(bf16[2048,32]{0,1:T(8,128)(2,1)} %param.8) | copy-start | bytes 393220
  1.0 0.7 copy-start.1

commit v9 on v7

--- a/solution.py
+++ b/solution.py
@@ -351,7 +351,7 @@
         scratch += [
             pltpu.VMEM((early, SPAN, norb), bf),
             pltpu.VMEM((early, npoints, SPAN), bf),
-            pltpu.VMEM((cols * LINES, LANES), jnp.float32),
+            pltpu.VMEM(((cols + 1) * LINES, LANES), jnp.float32),
             pltpu.SemaphoreType.DMA(()),
             pltpu.SemaphoreType.DMA((chunks,)),
         ]
@@ -527,7 +527,7 @@
         if turn:
             wide = pltpu.roll(wide, 2 * LANES - turn, 1)
         fit_rows[pl.ds(line, cols, stride=LINES), :] = wide[:, :LANES]
-    return fit_rows[...].astype(jnp.bfloat16).reshape(cols, LINES, LANES)
+    return fit_rows[: cols * LINES].astype(jnp.bfloat16).reshape(cols, LINES, LANES)
 
 
 def pair_fit_kernel(
@@ -670,7 +670,7 @@
         ],
         scratch_shapes=[
             pltpu.VMEM((cols, SPAN), jnp.float32),
-            pltpu.VMEM((cols * LINES, LANES), jnp.float32),
+            pltpu.VMEM(((cols + 1) * LINES, LANES), jnp.float32),
             pltpu.VMEM((2, cols, JOIN * LINES, LANES), bf),
             pltpu.SemaphoreType.DMA((2,)),
             pltpu.SemaphoreType.DMA((count,)),
@@ -803,7 +803,7 @@
         p = lax.dot_general(tyi_ref[...], both(rows), NN, preferred_element_type=f32).astype(bf)
         tall = jnp.concatenate([cut(p, k) for k in range(count)], axis=0)
         final = lax.dot_general(tall, tzi_ref[...], NN, preferred_element_type=f32)
-        flat[...] = final * f32(1.0 / float(NG**3))
+        flat[: count * NG] = final * f32(1.0 / float(NG**3))
         for k in range(count):
             y0, y1, y2, y3 = [flat[pl.ds(k * NG + j, quarter, stride=4), :] for j in range(4)]
             y1, y2, y3 = pltpu.roll(y1, 96, 1), pltpu.roll(y2, 64, 1), pltpu.roll(y3, 32, 1)
@@ -824,7 +824,7 @@
         own(piece).wait()
         others = land.at[piece, pl.ds(0, count - 1)]
         pltpu.make_async_copy(others, others, recv_sem.at[piece]).wait()
-        wide[...] = land[piece].astype(f32).reshape(cols * PIECE, LANES)
+        wide[: cols * PIECE] = land[piece].astype(f32).reshape(cols * PIECE, LANES)
         for half in range(per_piece):
             block = piece * per_piece + half
             slot = lax.rem(block, RING)
@@ -924,14 +924,14 @@
         out_specs=vmem_spec,
         scratch_shapes=[
             pltpu.VMEM((NG, NG, LANES), bf),
-            pltpu.VMEM((NG * NG, LANES), f32),
-            pltpu.VMEM((NG * NG, LANES), f32),
-            pltpu.VMEM((count * NG, LANES), f32),
-            pltpu.VMEM((4 * 3 * PIECE, LANES), f32),
+            pltpu.VMEM(((NG + 1) * NG, LANES), f32),
+            pltpu.VMEM(((NG + 1) * NG, LANES), f32),
+            pltpu.VMEM((count * NG + 8, LANES), f32),
+            pltpu.VMEM((4 * 3 * PIECE + 8, LANES), f32),
             pltpu.VMEM((pieces, count, PIECE, LANES), bf),
             pltpu.VMEM((RING, npoints, span), bf),
             pltpu.VMEM((pieces, count, PIECE, LANES), bf),
-            pltpu.VMEM((cols * PIECE, LANES), f32),
+            pltpu.VMEM(((cols + 1) * PIECE, LANES), f32),
             pltpu.VMEM((cols, npoints), f32),
             pltpu.VMEM((count, cols // 2, LANES), f32),
             pltpu.VMEM((count, cols // 2, LANES), f32),

time: 223 us -> 223 us (level)
  no operation moved by 1% of the time
where the time goes in v9:
time: 223 us; the launch traced here: 222 us
  Pallas kernels  219 us (98%)
    pallas_call x1, Pallas kernels, pair_and_fit(): pl.pallas_call(pair_fit_kernel, grid=(blocks,), in_specs=[pl.BlockSpec((S...  79.7 us
    pallas_call x1, Pallas kernels, solve_and_project(): pl.pallas_call(solve_project_kernel, out_shape=jax.ShapeDtypeStruct((cols...  73.6 us
    pallas_call x1, Pallas kernels, share_rows(): pl.pallas_call(body, out_shape=out_shape, in_specs=in_specs, out_specs=ou...  54.9 us
    pallas_call x1, Pallas kernels, pick_rows(): pl.pallas_call(pick_kernel, out_shape=jax.ShapeDtypeStruct((npoints, norb...  10.6 us

profile of v9, /device:TPU:0, one launch (start us, length us, event | category | flops | bytes accessed | tf_op | source)
XLA Modules:
  0.0 221.7 jit_solution(10905128584783816728)
XLA Ops:
  0.0 0.0 copy-start
  0.0 0.7 and_convert_fusion
  0.7 0.1 reshape.23
  0.8 0.1 reduce_max.9.flags_ref
  1.0 0.0 copy-start.1
  1.0 0.7 copy-done.1
  1.7 10.6 %pick_rows.1 = bf16[2048,512]{1,0:T(8,128)(2,1)S(1)} custom-call(s32[2048]{0:T(1024)S(1)} %copy-done.1, s32[256]{0:T(256)S(1)} %reduce_max.9.flags_ref, s32[1]{0:T(128)} %bitcast.offset_ref, bf16[3456,8,512]{2,1,0:T(8,128)(2,1)} %bitcast.12), custom_call_target="tpu_custom_call" | custom-call | tf_op jit(solution)/shard_map/pick_rows/pallas_call | solution.py:441
  12.2 0.0 copy-done
  12.2 54.9 %share_rows.1 = (bf16[4,2,4,4,16,512]{5,4,3,2,1,0:T(8,128)(2,1)S(1)}, bf16[4,2048,1536]{2,1,0:T(8,128)(2,1)}, bf16[32,48,128]{2,1,0:T(8,128)(2,1)S(1)}, f32[32,1536]{1,0:T(8,128)S(1)}) custom-call(bf16[4,2,4,4,16,512]{5,4,3,2,1,0:T(8,128)(2,1)S(1)} %bitcast.8, bf16[32,2048]{1,0:T(8,128)(2,1)S(1)} %bitcast.10, bf16[18,1536,512]{2,1,0:T(8,128)(2,1)} %bitcast.13), custom_call_target="tpu_custom_call" | custom-call | tf_op jit(solution)/shard_map/share_rows/pallas_call | solution.py:362
  67.1 79.7 %pair_fit_send.1 = (bf16[14,2048,1536]{2,1,0:T(8,128)(2,1)}, bf16[32,3,96,128]{3,2,1,0:T(8,128)(2,1)}) custom-call(bf16[27648,512]{1,0:T(8,128)(2,1)} %orb_ref.1, bf16[2048,512]{1,0:T(8,128)(2,1)S(1)} %bitcast.9, bf16[32,2048]{1,0:T(8,128)(2,1)S(1)} %bitcast.11, bf16[32,48,128]{2,1,0:T(8,128)(2,1)S(1)} %get-tuple-element.12.early_ref, ...), custom_call_target="tpu_custom_call" | custom-call | tf_op jit(solution)/shard_map/pair_fit_send/pallas_call | solution.py:653
  146.8 73.6 %solve_project.1 = f32[32,64]{1,0:T(8,128)} custom-call(bf16[96,96,128]{2,1,0:T(8,128)(2,1)} %bitcast.14, bf16[128,256]{1,0:T(8,128)(2,1)} %constant.26.clone.tz_ref, bf16[96,192]{1,0:T(8,128)(2,1)} %constant.27.clone.ty_ref, bf16[96,192]{1,0:T(8,128)(2,1)} %constant.28.clone.tyi_ref, bf16[128,128]{1,0:T(8,128)(2,1)} %constant.29.clone.tzi_ref, ...), custom_call_target="tpu_custom_call" | custom-call | tf_op jit(solution)/shard_map/solve_project/pallas_call | solution.py:920
  220.4 1.3 copy.9
Async XLA Ops:
  0.0 12.2 %copy-start = (bf16[2048,32]{0,1:T(8,128)(2,1)S(1)}, bf16[2048,32]{0,1:T(8,128)(2,1)}, u32[]{:S(2)}) copy-start(bf16[2048,32]{0,1:T(8,128)(2,1)} %param.8) | copy-start | bytes 393220
  1.0 0.7 copy-start.1
